TPU v7x, 32 devices: a whole 2x2x4 slice. The times are simulated.
32 devices in a mesh: basin: 2 (over x), dom: 8 (over z, y), hid: 2 (over core).
Axes of the slice: x: 2, y: 2, z: 4, core: 2. Of those that a mesh axis runs over, the one named last changes fastest.
Arguments:
- feats: bfloat16 [32768, 512], P(('basin', 'dom'), 'hid'), parts along dimension 0, may hold values from -6 to 6
- tiles: bfloat16 [256, 16, 128, 128], P(('basin', 'dom')), parts along dimension 0, may hold values from -0.125 to 0.125
- tile_cols: int32 [256, 16], P(('basin', 'dom')), parts along dimension 0, may hold values from 0 to 39, as said below
- sends: int32 [16, 3, 8], P(('basin', 'dom')), parts along dimension 0, may hold values from 0 to 15, as said below
- pins: int32 [16, 32], P(('basin', 'dom')), parts along dimension 0, may hold values from 0 to 2047, as said below
- weight: bfloat16 [512, 512], P(None, 'hid'), may hold values from -0.25 to 0.25
- bias: float32 [512], P('hid'), may hold values from -3 to 3
- cotan: bfloat16 [32768, 512], P(('basin', 'dom'), 'hid'), parts along dimension 0, may hold values from -6 to 6
Outputs:
- out: bfloat16 [32768, 512], P(('basin', 'dom'), 'hid'), parts along dimension 0
- dfeat: bfloat16 [32768, 512], P(('basin', 'dom'), 'hid'), parts along dimension 0
- dweight: float32 [1024, 512], P('basin', 'hid'), parts along dimension 0
- dbias: float32 [1024], P(('basin', 'hid')), parts along dimension 0
There are 2 independent parts, one for each index of `basin`. A program takes and returns all parts, laid end to end along the dimension named above; an argument that names none is the same for every part. Nothing has to cross between parts.
Inputs may be any that keep to these rules, and one draw needn't show every extreme that they name: `tile_cols`: every one of a partition's 40 sources is read by at least one of its tiles. `sends`: within one partition and matching the entries are distinct; every owned block of a partition is sent in some matching. `pins`: entries may repeat.
All inputs are finite; a program needn't handle non-finite values.
Results may differ from a plain program's by a relative error of at most 0.0054.
Values may be sent and summed in bfloat16 or wider, within the bound.
A program may use at most 128 MiB of HBM per device.

v0:
```python
import math

import jax
import jax.numpy as jnp
from jax import lax
from jax.sharding import PartitionSpec as P


def swapped(block, axis, distance):
    count = lax.axis_size(axis)
    route = []
    for low in range(count):
        high = low | 1 << distance
        if high != low and high < count:
            route += [(low, high), (high, low)]
    return lax.ppermute(block, axis, route)


def body(feats, tiles, tile_cols, sends, pins, weight, bias, cotan):
    rows, width = feats.shape
    nblock = rows // 128
    nsend = sends.shape[2]
    ntile = tiles.shape[1]
    parts = lax.axis_size("dom")
    nbits = parts.bit_length() - 1
    shifts = (0, nbits // 2, nbits - 1)
    blocks = feats.reshape(nblock, 128, width)
    received = []
    for m in range(3):
        picked = blocks[sends[0, m]]
        received.append(swapped(picked, "dom", shifts[m]))
    sources = jnp.concatenate([blocks] + received, axis=0)
    selected = sources[tile_cols]
    agg = jnp.einsum("rkij,rkjh->rih", tiles, selected, preferred_element_type=jnp.float32)
    agg = agg.astype(jnp.bfloat16).reshape(rows, width)
    whole_agg = lax.all_gather(agg, "hid", axis=1, tiled=True)
    pre = jnp.dot(whole_agg, weight, preferred_element_type=jnp.float32) + bias
    local_ids = jnp.arange(rows, dtype=jnp.int32)
    pinned = jnp.any(local_ids[:, None] == pins[0][None, :], axis=1)
    keep = 1.0 - pinned.astype(jnp.float32)
    sig = jax.nn.sigmoid(pre)
    out = (feats.astype(jnp.float32) + keep[:, None] * pre * sig).astype(jnp.bfloat16)
    dpre = (keep[:, None] * cotan.astype(jnp.float32) * sig * (1.0 + pre * (1.0 - sig))).astype(
        jnp.bfloat16
    )
    scale = 1.0 / math.sqrt(parts * rows)
    weight_term = lax.dot_general(
        whole_agg, dpre, (((0,), (0,)), ((), ())), preferred_element_type=jnp.float32
    )
    bias_term = jnp.sum(dpre.astype(jnp.float32), axis=0)
    full_dpre, full_weight = (
        lax.all_gather(dpre, "hid", axis=1, tiled=True),
        lax.all_gather(weight, "hid", axis=1, tiled=True),
    )
    start = lax.axis_index("hid") * width
    weight_rows = lax.dynamic_slice_in_dim(full_weight, start, width, 0)
    dagg = lax.dot_general(
        full_dpre, weight_rows, (((1,), (1,)), ((), ())), preferred_element_type=jnp.float32
    ).astype(jnp.bfloat16)
    summed_weight, summed_bias = lax.psum((weight_term, bias_term), "dom")
    dweight = summed_weight * scale
    dbias = summed_bias * scale
    dblocks = dagg.reshape(nblock, 128, width)
    count = sources.shape[0]

    def add_slot(slot, total):
        tile_slot = lax.dynamic_index_in_dim(tiles, slot, 1, keepdims=False)
        col_slot = lax.dynamic_index_in_dim(tile_cols, slot, 1, keepdims=False)
        term = jnp.einsum("rij,rih->rjh", tile_slot, dblocks, preferred_element_type=jnp.float32)
        return total.at[col_slot].add(term)

    dsrc = lax.fori_loop(0, ntile, add_slot, jnp.zeros((count, 128, width), jnp.float32))
    own = dsrc[:nblock]
    for m in range(3):
        outgoing = dsrc[nblock + m * nsend : nblock + (m + 1) * nsend]
        back = swapped(outgoing, "dom", shifts[m])
        own = own.at[sends[0, m]].add(back)
    dfeat = (cotan.astype(jnp.float32) + own.reshape(rows, width)).astype(jnp.bfloat16)
    return (out, dfeat, dweight, dbias)


def solution(mesh):
    return jax.shard_map(
        body,
        mesh=mesh,
        in_specs=(
            P(("basin", "dom"), "hid"),
            P(("basin", "dom"), None, None, None),
            P(("basin", "dom"), None),
            P(("basin", "dom"), None, None),
            P(("basin", "dom"), None),
            P(None, "hid"),
            P("hid"),
            P(("basin", "dom"), "hid"),
        ),
        out_specs=(
            P(("basin", "dom"), "hid"),
            P(("basin", "dom"), "hid"),
            P("basin", "hid"),
            P(("basin", "hid")),
        ),
        check_vma=False,
    )
```

profile of v0, /device:TPU:0, one launch (start us, length us, event | category | flops | bytes accessed | tf_op | source)
XLA Modules:
  0.0 328.6 jit_solution(1892276636165411303)
XLA Ops:
  8.0 1.8 gather_fusion
  9.8 3.0 collective-permute-start
  12.9 1.8 gather_fusion.1
  14.7 1.6 collective-permute-start.1
  16.3 1.4 gather_fusion.2
  17.7 2.6 collective-permute-start.2
  20.4 4.4 %collective-permute-done = bf16[8,128,256]{2,1,0:T(8,128)(2,1)S(1)} collective-permute-done((bf16[8,128,256]{2,1,0:T(8,128)(2,1)S(1)}, bf16[8,128,256]{2,1,0:T(8,128)(2,1)S(1)}, u32[]{:S(2)}, u32[]{:S(2)}) %collective-permute-start) | collective-permute-done | bytes 524320 | tf_op jit(solution)/shard_map/ppermute | solution.py:16
  24.8 12.9 %collective-permute-done.1 = bf16[8,128,256]{2,1,0:T(8,128)(2,1)S(1)} collective-permute-done((bf16[8,128,256]{2,1,0:T(8,128)(2,1)S(1)}, bf16[8,128,256]{2,1,0:T(8,128)(2,1)S(1)}, u32[]{:S(2)}, u32[]{:S(2)}) %collective-permute-start.1) | collective-permute-done | bytes 524320 | tf_op jit(solution)/shard_map/ppermute | solution.py:16
  38.4 4.9 %collective-permute-done.2 = bf16[8,128,256]{2,1,0:T(8,128)(2,1)} collective-permute-done((bf16[8,128,256]{2,1,0:T(8,128)(2,1)}, bf16[8,128,256]{2,1,0:T(8,128)(2,1)}, u32[]{:S(2)}, u32[]{:S(2)}) %collective-permute-start.2) | collective-permute-done | bytes 524320 | tf_op jit(solution)/shard_map/ppermute | solution.py:16
  43.3 1.7 pad_maximum_fusion
  45.0 9.8 %gather_fusion.3 = bf16[256,128,256]{2,1,0:T(8,128)(2,1)} fusion(bf16[40,128,256]{2,1,0:T(8,128)(2,1)S(1)} %pad_maximum_fusion, s32[1024]{0:T(1024)S(1)} %pad_clamp_fusion), kind=kCustom, calls=%fused_computation.3 | custom fusion | bytes 33555456 | tf_op jit(solution)/shard_map/gather | solution.py:33
  54.8 11.9 %bitcast_convert_fusion = bf16[16,256,128]{1,2,0:T(8,128)(2,1)} fusion(bf16[16,16,128,128]{3,2,1,0:T(8,128)(2,1)} %param.11, bf16[16,16,128,256]{3,2,1,0:T(8,128)(2,1)} %bitcast.44), kind=kOutput, calls=%fused_computation.23 | convolution fusion | flops 2148007936 | bytes 26214400 | tf_op jit(solution)/shard_map/rkij,rkjh->rih/dot_general | solution.py:34
  66.9 9.4 %all-gather.3.cloned.1.call-done = bf16[2048,512]{1,0:T(8,128)(2,1)} async-done(((bf16[2048,256]{1,0:T(8,128)(2,1)}), bf16[2048,512]{1,0:T(8,128)(2,1)}) %all-gather.3.cloned.1.call-update) | async-done | bytes 2097168 | tf_op jit(solution)/shard_map/all_gather | solution.py:36
  76.4 4.4 %convert_reduce_fusion = (f32[256]{0:T(256)S(1)}, bf16[2048,256]{1,0:T(8,128)(2,1)}, bf16[2048,256]{1,0:T(8,128)(2,1)}) fusion(bf16[2048,256]{1,0:T(8,128)(2,1)S(1)} %copy-done.4, f32[2048]{0:T(1024)S(1)} %convert_subtract_fusion, bf16[2048,256]{1,0:T(8,128)(2,1)S(1)} %copy-done.1, f32[256]{0:T(256)S(1)} %copy-done.9, ...), kind=kOutput, calls=%fused_computation.24 | convolution fusion | flops 546832128 | bytes 6563840 | tf_op jit(solution)/shard_map/dot_general | solution.py:37
  80.9 2.2 all_gather.11
  83.1 9.4 %all-gather.5.cloned.1.call-done = bf16[2048,512]{1,0:T(8,128)(2,1)} async-done(((bf16[2048,256]{1,0:T(8,128)(2,1)}), bf16[2048,512]{1,0:T(8,128)(2,1)}) %all-gather.5.cloned.1.call-update) | async-done | bytes 2097168 | tf_op jit(solution)/shard_map/all_gather | solution.py:52
  92.5 2.3 convolution_convert_fusion
  94.8 2.9 broadcast_in_dim.7
  97.7 96.9 %while.13 = (s32[]{:T(128)}, f32[40,128,256]{2,1,0:T(8,128)}, s32[16,16]{0,1:T(8,128)S(1)}, bf16[16,16,128,128]{3,2,1,0:T(8,128)(2,1)}, bf16[16,128,256]{2,1,0:T(8,128)(2,1)S(1)}, /*index=5*/s32[]{:T(128)}) while((s32[]{:T(128)}, f32[40,128,256]{2,1,0:T(8,128)}, s32[16,16]{0,1:T(8,128)S(1)}, bf16[16,16,128,128]{3,2,1,0:T(8,128)(2,1)}, ...), condition=%wide.region_3.0_spmd, body=%wide.region_1.3_spmd.sunk | while | flops 134742064 | bytes 9962249 | solution.py:72
  97.7 1.5 fusion.33
  99.3 4.5 %scatter_fusion = f32[40,128,256]{2,1,0:T(8,128)} fusion(f32[40,128,256]{2,1,0:T(8,128)} %get-tuple-element.166, s32[16]{0:T(128)S(1)} %fusion.32, f32[16,128,256]{2,1,0:T(8,128)S(1)} %fusion.33), kind=kCustom, calls=%fused_computation.4.clone.1 | custom fusion | flops 524288 | bytes 6291520 | tf_op jit(solution)/shard_map/while/body/eval_jaxpr/scatter-add | solution.py:70
  103.8 1.5 fusion.33
  105.3 4.5 %scatter_fusion = f32[40,128,256]{2,1,0:T(8,128)} fusion(f32[40,128,256]{2,1,0:T(8,128)} %get-tuple-element.166, s32[16]{0:T(128)S(1)} %fusion.32, f32[16,128,256]{2,1,0:T(8,128)S(1)} %fusion.33), kind=kCustom, calls=%fused_computation.4.clone.1 | custom fusion | flops 524288 | bytes 6291520 | tf_op jit(solution)/shard_map/while/body/eval_jaxpr/scatter-add | solution.py:70
  109.8 1.5 fusion.33
  111.3 4.5 %scatter_fusion = f32[40,128,256]{2,1,0:T(8,128)} fusion(f32[40,128,256]{2,1,0:T(8,128)} %get-tuple-element.166, s32[16]{0:T(128)S(1)} %fusion.32, f32[16,128,256]{2,1,0:T(8,128)S(1)} %fusion.33), kind=kCustom, calls=%fused_computation.4.clone.1 | custom fusion | flops 524288 | bytes 6291520 | tf_op jit(solution)/shard_map/while/body/eval_jaxpr/scatter-add | solution.py:70
  115.9 1.5 fusion.33
  117.4 4.5 %scatter_fusion = f32[40,128,256]{2,1,0:T(8,128)} fusion(f32[40,128,256]{2,1,0:T(8,128)} %get-tuple-element.166, s32[16]{0:T(128)S(1)} %fusion.32, f32[16,128,256]{2,1,0:T(8,128)S(1)} %fusion.33), kind=kCustom, calls=%fused_computation.4.clone.1 | custom fusion | flops 524288 | bytes 6291520 | tf_op jit(solution)/shard_map/while/body/eval_jaxpr/scatter-add | solution.py:70
  121.9 1.5 fusion.33
  123.5 4.6 %scatter_fusion = f32[40,128,256]{2,1,0:T(8,128)} fusion(f32[40,128,256]{2,1,0:T(8,128)} %get-tuple-element.166, s32[16]{0:T(128)S(1)} %fusion.32, f32[16,128,256]{2,1,0:T(8,128)S(1)} %fusion.33), kind=kCustom, calls=%fused_computation.4.clone.1 | custom fusion | flops 524288 | bytes 6291520 | tf_op jit(solution)/shard_map/while/body/eval_jaxpr/scatter-add | solution.py:70
  128.1 1.5 fusion.33
  129.6 4.5 %scatter_fusion = f32[40,128,256]{2,1,0:T(8,128)} fusion(f32[40,128,256]{2,1,0:T(8,128)} %get-tuple-element.166, s32[16]{0:T(128)S(1)} %fusion.32, f32[16,128,256]{2,1,0:T(8,128)S(1)} %fusion.33), kind=kCustom, calls=%fused_computation.4.clone.1 | custom fusion | flops 524288 | bytes 6291520 | tf_op jit(solution)/shard_map/while/body/eval_jaxpr/scatter-add | solution.py:70
  134.2 1.5 fusion.33
  135.7 4.4 %scatter_fusion = f32[40,128,256]{2,1,0:T(8,128)} fusion(f32[40,128,256]{2,1,0:T(8,128)} %get-tuple-element.166, s32[16]{0:T(128)S(1)} %fusion.32, f32[16,128,256]{2,1,0:T(8,128)S(1)} %fusion.33), kind=kCustom, calls=%fused_computation.4.clone.1 | custom fusion | flops 524288 | bytes 6291520 | tf_op jit(solution)/shard_map/while/body/eval_jaxpr/scatter-add | solution.py:70
  140.1 1.5 fusion.33
  141.7 4.4 %scatter_fusion = f32[40,128,256]{2,1,0:T(8,128)} fusion(f32[40,128,256]{2,1,0:T(8,128)} %get-tuple-element.166, s32[16]{0:T(128)S(1)} %fusion.32, f32[16,128,256]{2,1,0:T(8,128)S(1)} %fusion.33), kind=kCustom, calls=%fused_computation.4.clone.1 | custom fusion | flops 524288 | bytes 6291520 | tf_op jit(solution)/shard_map/while/body/eval_jaxpr/scatter-add | solution.py:70
  146.1 1.5 fusion.33
  147.7 4.5 %scatter_fusion = f32[40,128,256]{2,1,0:T(8,128)} fusion(f32[40,128,256]{2,1,0:T(8,128)} %get-tuple-element.166, s32[16]{0:T(128)S(1)} %fusion.32, f32[16,128,256]{2,1,0:T(8,128)S(1)} %fusion.33), kind=kCustom, calls=%fused_computation.4.clone.1 | custom fusion | flops 524288 | bytes 6291520 | tf_op jit(solution)/shard_map/while/body/eval_jaxpr/scatter-add | solution.py:70
  152.2 1.5 fusion.33
  153.7 4.4 %scatter_fusion = f32[40,128,256]{2,1,0:T(8,128)} fusion(f32[40,128,256]{2,1,0:T(8,128)} %get-tuple-element.166, s32[16]{0:T(128)S(1)} %fusion.32, f32[16,128,256]{2,1,0:T(8,128)S(1)} %fusion.33), kind=kCustom, calls=%fused_computation.4.clone.1 | custom fusion | flops 524288 | bytes 6291520 | tf_op jit(solution)/shard_map/while/body/eval_jaxpr/scatter-add | solution.py:70
  158.2 1.5 fusion.33
  159.7 4.5 %scatter_fusion = f32[40,128,256]{2,1,0:T(8,128)} fusion(f32[40,128,256]{2,1,0:T(8,128)} %get-tuple-element.166, s32[16]{0:T(128)S(1)} %fusion.32, f32[16,128,256]{2,1,0:T(8,128)S(1)} %fusion.33), kind=kCustom, calls=%fused_computation.4.clone.1 | custom fusion | flops 524288 | bytes 6291520 | tf_op jit(solution)/shard_map/while/body/eval_jaxpr/scatter-add | solution.py:70
  164.2 1.5 fusion.33
  165.8 4.6 %scatter_fusion = f32[40,128,256]{2,1,0:T(8,128)} fusion(f32[40,128,256]{2,1,0:T(8,128)} %get-tuple-element.166, s32[16]{0:T(128)S(1)} %fusion.32, f32[16,128,256]{2,1,0:T(8,128)S(1)} %fusion.33), kind=kCustom, calls=%fused_computation.4.clone.1 | custom fusion | flops 524288 | bytes 6291520 | tf_op jit(solution)/shard_map/while/body/eval_jaxpr/scatter-add | solution.py:70
  170.3 1.5 fusion.33
  171.9 4.6 %scatter_fusion = f32[40,128,256]{2,1,0:T(8,128)} fusion(f32[40,128,256]{2,1,0:T(8,128)} %get-tuple-element.166, s32[16]{0:T(128)S(1)} %fusion.32, f32[16,128,256]{2,1,0:T(8,128)S(1)} %fusion.33), kind=kCustom, calls=%fused_computation.4.clone.1 | custom fusion | flops 524288 | bytes 6291520 | tf_op jit(solution)/shard_map/while/body/eval_jaxpr/scatter-add | solution.py:70
  176.5 1.5 fusion.33
  178.0 4.6 %scatter_fusion = f32[40,128,256]{2,1,0:T(8,128)} fusion(f32[40,128,256]{2,1,0:T(8,128)} %get-tuple-element.166, s32[16]{0:T(128)S(1)} %fusion.32, f32[16,128,256]{2,1,0:T(8,128)S(1)} %fusion.33), kind=kCustom, calls=%fused_computation.4.clone.1 | custom fusion | flops 524288 | bytes 6291520 | tf_op jit(solution)/shard_map/while/body/eval_jaxpr/scatter-add | solution.py:70
  182.6 1.5 fusion.33
  184.1 4.4 %scatter_fusion = f32[40,128,256]{2,1,0:T(8,128)} fusion(f32[40,128,256]{2,1,0:T(8,128)} %get-tuple-element.166, s32[16]{0:T(128)S(1)} %fusion.32, f32[16,128,256]{2,1,0:T(8,128)S(1)} %fusion.33), kind=kCustom, calls=%fused_computation.4.clone.1 | custom fusion | flops 524288 | bytes 6291520 | tf_op jit(solution)/shard_map/while/body/eval_jaxpr/scatter-add | solution.py:70
  188.6 1.5 fusion.33
  190.1 4.6 %scatter_fusion = f32[40,128,256]{2,1,0:T(8,128)} fusion(f32[40,128,256]{2,1,0:T(8,128)} %get-tuple-element.166, s32[16]{0:T(128)S(1)} %fusion.32, f32[16,128,256]{2,1,0:T(8,128)S(1)} %fusion.33), kind=kCustom, calls=%fused_computation.4.clone.1 | custom fusion | flops 524288 | bytes 6291520 | tf_op jit(solution)/shard_map/while/body/eval_jaxpr/scatter-add | solution.py:70
  194.7 3.7 %fusion.16 = (f32[8,128,256]{2,1,0:T(8,128)}, f32[8,128,256]{2,1,0:T(8,128)}, f32[8,128,256]{2,1,0:T(8,128)}) fusion(f32[40,128,256]{2,1,0:T(8,128)} %get-tuple-element.98), kind=kLoop, calls=%fused_computation.45 | loop fusion | bytes 6291456 | tf_op jit(solution)/shard_map/slice | solution.py:75
  198.4 1.7 collective-permute-start.3
  200.1 1.4 collective-permute-start.4
  201.5 2.8 collective-permute-start.5
  204.3 1.5 fusion.17
  205.9 61.5 %psum.15 = f32[256]{0:T(256)S(1)} all-reduce(f32[256]{0:T(256)S(1)} %get-tuple-element.119), channel_id=1, replica_groups=mesh['basin'=2,'dom'=8,'hid'=2] {'dom'}, use_global_device_ids=true, to_apply=%region_9.10 | all-reduce | flops 256 | bytes 2048 | tf_op jit(solution)/shard_map/psum | solution.py:60
  267.9 41.7 %all-reduce.2.cloned.1.call-done = f32[512,256]{1,0:T(8,128)} async-done(((f32[512,256]{1,0:T(8,128)}), f32[512,256]{1,0:T(8,128)}) %all-reduce.2.cloned.1.call-update) | async-done | bytes 524304 | tf_op jit(solution)/shard_map/psum | solution.py:60
  309.6 1.9 broadcast_multiply_fusion
  311.5 1.8 slice.27
  313.3 2.5 scatter_fusion.1
  315.8 2.5 scatter_fusion.2
  318.3 1.3 scatter_fusion.3
  319.7 2.5 fusion.8
  (56 shorter events, 2.9 us)
Async XLA Ops:
  7.2 9.2 %copy-start = (bf16[2048,256]{1,0:T(8,128)(2,1)S(1)}, bf16[2048,256]{1,0:T(8,128)(2,1)}, u32[]{:S(2)}) copy-start(bf16[2048,256]{1,0:T(8,128)(2,1)} %param.10) | copy-start | bytes 3145732
  7.2 13.1 %copy-start.7 = (s32[16,16]{1,0:T(8,128)S(1)}, s32[16,16]{1,0:T(8,128)}, u32[]{:S(2)}) copy-start(s32[16,16]{1,0:T(8,128)} %param.12) | copy-start | bytes 3076
  7.2 69.2 %all-gather.3.cloned.1.call-start = ((), (), s32[]{:S(2)}) async-start(), calls=%async_computation | async-start | bytes 3145728 | tf_op jit(solution)/shard_map/all_gather | solution.py:36
  9.8 15.0 %collective-permute-start = (bf16[8,128,256]{2,1,0:T(8,128)(2,1)S(1)}, bf16[8,128,256]{2,1,0:T(8,128)(2,1)S(1)}, u32[]{:S(2)}, u32[]{:S(2)}) collective-permute-start(bf16[8,128,256]{2,1,0:T(8,128)(2,1)S(1)} %gather_fusion), channel_id=1, source_target_pairs={{0,2},{2,0},{4,6},{6,4},{8,10},{10,8},{12,14},{14,12},{1,3},{3,1},... | collective-permute-start | bytes 1572872 | tf_op jit(solution)/shard_map/ppermute | solution.py:16
  14.7 23.0 %collective-permute-start.1 = (bf16[8,128,256]{2,1,0:T(8,128)(2,1)S(1)}, bf16[8,128,256]{2,1,0:T(8,128)(2,1)S(1)}, u32[]{:S(2)}, u32[]{:S(2)}) collective-permute-start(bf16[8,128,256]{2,1,0:T(8,128)(2,1)S(1)} %gather_fusion.1), channel_id=1, source_target_pairs={{0,4},{4,0},{2,6},{6,2},{8,12},{12,8},{10,14},{14,10},{1,5},{5,1},... | collective-permute-start | bytes 1572872 | tf_op jit(solution)/shard_map/ppermute | solution.py:16
  17.7 25.6 %collective-permute-start.2 = (bf16[8,128,256]{2,1,0:T(8,128)(2,1)}, bf16[8,128,256]{2,1,0:T(8,128)(2,1)}, u32[]{:S(2)}, u32[]{:S(2)}) collective-permute-start(bf16[8,128,256]{2,1,0:T(8,128)(2,1)} %gather_fusion.2), channel_id=1, source_target_pairs={{0,8},{8,0},{2,10},{10,2},{4,12},{12,4},{6,14},{14,6},{1,9},{9,1},... | collective-permute-start | bytes 1572872 | tf_op jit(solution)/shard_map/ppermute | solution.py:16
  37.7 0.8 copy-start.5
  54.8 12.0 %copy-start.8 = (s32[1,32]{1,0:T(1,128)S(1)}, s32[1,32]{1,0:T(1,128)}, u32[]{:S(2)}) copy-start(s32[1,32]{1,0:T(1,128)} %param.14) | copy-start | bytes 388
  54.8 21.6 %copy-start.1 = (bf16[2048,256]{1,0:T(8,128)(2,1)S(1)}, bf16[2048,256]{1,0:T(8,128)(2,1)}, u32[]{:S(2)}) copy-start(bf16[2048,256]{1,0:T(8,128)(2,1)} %param.10) | copy-start | bytes 3145732
  54.8 21.6 %copy-start.4 = (bf16[2048,256]{1,0:T(8,128)(2,1)S(1)}, bf16[2048,256]{1,0:T(8,128)(2,1)}, u32[]{:S(2)}) copy-start(bf16[2048,256]{1,0:T(8,128)(2,1)} %param.17) | copy-start | bytes 3145732
  54.8 21.6 %copy-start.6 = (bf16[512,256]{1,0:T(8,128)(2,1)S(1)}, bf16[512,256]{1,0:T(8,128)(2,1)}, u32[]{:S(2)}) copy-start(bf16[512,256]{1,0:T(8,128)(2,1)} %param.15) | copy-start | bytes 786436
  54.8 21.6 %copy-start.9 = (f32[256]{0:T(256)S(1)}, f32[256]{0:T(256)}, u32[]{:S(2)}) copy-start(f32[256]{0:T(256)} %param.16) | copy-start | bytes 3076
  66.8 25.7 %all-gather.5.cloned.1.call-start = ((), (), s32[]{:S(2)}) async-start(), calls=%async_computation.1 | async-start | bytes 3145728 | tf_op jit(solution)/shard_map/all_gather | solution.py:52
  80.8 228.8 %all-reduce.2.cloned.1.call-start = ((), (), s32[]{:S(2)}) async-start(), calls=%async_computation.2 | async-start | bytes 1048576 | tf_op jit(solution)/shard_map/psum | solution.py:60
  194.7 9.6 %copy-start.2 = (bf16[2048,256]{1,0:T(8,128)(2,1)S(1)}, bf16[2048,256]{1,0:T(8,128)(2,1)}, u32[]{:S(2)}) copy-start(bf16[2048,256]{1,0:T(8,128)(2,1)} %get-tuple-element.120) | copy-start | bytes 3145732
  194.7 9.6 %copy-start.3 = (bf16[2048,512]{1,0:T(8,128)(2,1)S(1)}, bf16[2048,512]{1,0:T(8,128)(2,1)}, u32[]{:S(2)}) copy-start(bf16[2048,512]{1,0:T(8,128)(2,1)} %all-gather.3.cloned.1.call-done) | copy-start | bytes 6291460
  198.4 114.9 %collective-permute-start.3 = (f32[8,128,256]{2,1,0:T(8,128)}, f32[8,128,256]{2,1,0:T(8,128)}, u32[]{:S(2)}, u32[]{:S(2)}) collective-permute-start(f32[8,128,256]{2,1,0:T(8,128)} %get-tuple-element.123), channel_id=1, source_target_pairs={{0,2},{2,0},{4,6},{6,4},{8,10},{10,8},{12,14},{14,12},{1,3},{3,1},... | collective-permute-start | bytes 3145736 | tf_op jit(solution)/shard_map/ppermute | solution.py:16
  200.1 115.7 %collective-permute-start.4 = (f32[8,128,256]{2,1,0:T(8,128)}, f32[8,128,256]{2,1,0:T(8,128)}, u32[]{:S(2)}, u32[]{:S(2)}) collective-permute-start(f32[8,128,256]{2,1,0:T(8,128)} %get-tuple-element.122), channel_id=1, source_target_pairs={{0,4},{4,0},{2,6},{6,2},{8,12},{12,8},{10,14},{14,10},{1,5},{5,1},... | collective-permute-start | bytes 3145736 | tf_op jit(solution)/shard_map/ppermute | solution.py:16
  201.5 116.8 %collective-permute-start.5 = (f32[8,128,256]{2,1,0:T(8,128)}, f32[8,128,256]{2,1,0:T(8,128)S(1)}, u32[]{:S(2)}, u32[]{:S(2)}) collective-permute-start(f32[8,128,256]{2,1,0:T(8,128)} %get-tuple-element.121), channel_id=1, source_target_pairs={{0,8},{8,0},{2,10},{10,2},{4,12},{12,4},{6,14},{14,6},{1,9},{9,1},... | collective-permute-start | bytes 3145736 | tf_op jit(solution)/shard_map/ppermute | solution.py:16
Sparse Core Ops, SparseCore 0:
  66.9 9.4 all-gather.2
  80.9 11.5 all-gather.4
  206.0 103.5 all-reduce.1
where the time goes:
time: 330 us; the launch traced here: 329 us
  other arithmetic  86.2 us (26%)
  waiting for transfers between devices  82.7 us (25%)
  blocking collectives  63.6 us (19%)
  matrix products  44.6 us (14%)
  local copies, waits for them, and re-layouts  24.2 us (7%)
  between operations  13.9 us (4%)
  starting transfers between devices  13.3 us (4%)
    scatter-add x16, other arithmetic, add_slot(): return total.at[col_slot].add(term)  72.1 us
    psum x1, blocking collectives, body(): summed_weight, summed_bias = lax.psum((weight_term, bias_term), 'dom')  61.5 us
    psum x1, waiting for transfers between devices, body(): summed_weight, summed_bias = lax.psum((weight_term, bias_term), 'dom')  41.7 us
    dot_general x16, matrix products, add_slot(): jnp.einsum('rij,rih->rjh', tile_slot, dblocks, preferred_element_type=jnp...  24.4 us
    ppermute x6, waiting for transfers between devices, swapped(): return lax.ppermute(block, axis, route)  22.1 us
    ppermute x6, starting transfers between devices, swapped(): return lax.ppermute(block, axis, route)  13.1 us
    dot_general x1, matrix products, body(): jnp.einsum('rkij,rkjh->rih', tiles, selected, preferred_element_type=jnp....  11.9 us
    gather x1, local copies, waits for them, and re-layouts, body(): selected = sources[tile_cols]  9.76 us
  transfers between devices with their start and end apart: 9, of which 6 were waited for; matrix products, arithmetic and copies ran while one was open for 4% of the time, Pallas kernels for 0%

commit v1 on v0

v1 whole, which is shorter than its diff:
```python
import functools
import math

import jax
import jax.numpy as jnp
from jax import lax
from jax.experimental import pallas as pl
from jax.experimental.pallas import tpu as pltpu
from jax.sharding import PartitionSpec as P

BLK = 128
VMEM = pltpu.VMEM


def swapped(block, axis, distance):
    count = lax.axis_size(axis)
    route = []
    for low in range(count):
        high = low | 1 << distance
        if high != low and high < count:
            route += [(low, high), (high, low)]
    return lax.ppermute(block, axis, route)


def whole(shape):
    return pl.BlockSpec(shape, lambda *_: (0,) * len(shape))


def params(mib, count=1):
    return pltpu.CompilerParams(
        vmem_limit_bytes=mib << 20, dimension_semantics=("arbitrary",) * count
    )


def pick_kernel(nsend, sends_ref, feats_ref, *out_refs):
    for m in range(3):
        for j in range(nsend):
            out_refs[m][j] = feats_ref[sends_ref[m * nsend + j]]


def pick_call(blocks, sends):
    nblock, _, width = blocks.shape
    nsend = sends.shape[2]
    return pl.pallas_call(
        functools.partial(pick_kernel, nsend),
        grid_spec=pltpu.PrefetchScalarGridSpec(
            num_scalar_prefetch=1,
            grid=(1,),
            in_specs=[whole((nblock, BLK, width))],
            out_specs=[whole((nsend, BLK, width))] * 3,
        ),
        out_shape=[jax.ShapeDtypeStruct((nsend, BLK, width), blocks.dtype)] * 3,
        compiler_params=params(16),
        name="pick",
    )(sends.reshape(-1), blocks)


def agg_kernel(ntile, nblock, nsend, cols_ref, tiles_ref, own_ref, r0, r1, r2, agg_ref, src, sems):
    r = pl.program_id(0)

    @pl.when(r == 0)
    def _():
        copies = [pltpu.make_async_copy(own_ref, src.at[pl.ds(0, nblock)], sems.at[0])]
        for m, ref in enumerate((r0, r1, r2)):
            copies.append(
                pltpu.make_async_copy(
                    ref, src.at[pl.ds(nblock + m * nsend, nsend)], sems.at[m + 1]
                )
            )
        for copy in copies:
            copy.start()
        for copy in copies:
            copy.wait()

    lhs = jnp.concatenate([tiles_ref[0, k] for k in range(ntile)], axis=1)
    rhs = jnp.concatenate([src[cols_ref[r * ntile + k]] for k in range(ntile)], axis=0)
    agg_ref[...] = jnp.dot(lhs, rhs, preferred_element_type=jnp.float32).astype(agg_ref.dtype)


def agg_call(tiles, cols, blocks, received):
    nblock, ntile = tiles.shape[:2]
    width = blocks.shape[2]
    nsend = received[0].shape[0]
    anywhere = pl.BlockSpec(memory_space=pl.ANY)
    return pl.pallas_call(
        functools.partial(agg_kernel, ntile, nblock, nsend),
        grid_spec=pltpu.PrefetchScalarGridSpec(
            num_scalar_prefetch=1,
            grid=(nblock,),
            in_specs=[pl.BlockSpec((1, ntile, BLK, BLK), lambda r, _: (r, 0, 0, 0))]
            + [anywhere] * 4,
            out_specs=pl.BlockSpec((BLK, width), lambda r, _: (r, 0)),
            scratch_shapes=[
                VMEM((nblock + 3 * nsend, BLK, width), blocks.dtype),
                pltpu.SemaphoreType.DMA((4,)),
            ],
        ),
        out_shape=jax.ShapeDtypeStruct((nblock * BLK, width), blocks.dtype),
        compiler_params=params(24),
        name="agg",
    )(cols, tiles, blocks, *received)


TRANS = (((1,), (1,)), ((), ()))
DEEP = (((0,), (0,)), ((), ()))


def mid_kernel(mine_ref, other_ref, w_ref, bias_ref, pins_ref, feats_ref, cotan_ref, out_ref, dpre_ref, wb_ref):
    step = pl.program_id(0)
    chunk, width = feats_ref.shape
    hid = lax.axis_index("hid")
    here = pl.ds(pl.multiple_of(hid * width, width), width)
    there = pl.ds(pl.multiple_of((1 - hid) * width, width), width)
    mine, other = mine_ref[...], other_ref[...]
    pre = (
        jnp.dot(mine, w_ref[here, :], preferred_element_type=jnp.float32)
        + jnp.dot(other, w_ref[there, :], preferred_element_type=jnp.float32)
        + bias_ref[...]
    )
    ids = lax.broadcasted_iota(jnp.int32, (chunk, pins_ref.shape[1]), 0) + step * chunk
    hit = jnp.where(ids == pins_ref[...], 1.0, 0.0)
    keep = 1.0 - jnp.max(hit, axis=1, keepdims=True)
    sig = jax.nn.sigmoid(pre)
    out_ref[...] = (feats_ref[...].astype(jnp.float32) + keep * pre * sig).astype(out_ref.dtype)
    dpre = (
        keep * cotan_ref[...].astype(jnp.float32) * sig * (1.0 + pre * (1.0 - sig))
    ).astype(dpre_ref.dtype)
    dpre_ref[...] = dpre

    @pl.when(step == 0)
    def _():
        wb_ref[...] = jnp.zeros_like(wb_ref)

    wb_ref[here, :] += lax.dot_general(mine, dpre, DEEP, preferred_element_type=jnp.float32)
    wb_ref[there, :] += lax.dot_general(other, dpre, DEEP, preferred_element_type=jnp.float32)
    folded = jnp.sum(dpre.astype(jnp.float32).reshape(chunk // 8, 8, width), axis=0)
    wb_ref[2 * width :, :] += folded


def mid_call(mine, other, weight, bias, pins, feats, cotan):
    rows, width = feats.shape
    chunk = 256
    rowed = pl.BlockSpec((chunk, width), lambda i: (i, 0))
    return pl.pallas_call(
        mid_kernel,
        grid=(rows // chunk,),
        in_specs=[
            rowed,
            rowed,
            whole(weight.shape),
            whole((1, width)),
            whole(pins.shape),
            rowed,
            rowed,
        ],
        out_specs=[rowed, rowed, whole((2 * width + 8, width))],
        out_shape=[
            jax.ShapeDtypeStruct((rows, width), feats.dtype),
            jax.ShapeDtypeStruct((rows, width), feats.dtype),
            jax.ShapeDtypeStruct((2 * width + 8, width), jnp.float32),
        ],
        compiler_params=params(24),
        name="mid",
    )(mine, other, weight, bias.reshape(1, width), pins, feats, cotan)


def spread_kernel(ntile, nblock, cols_ref, tiles_ref, mine_ref, other_ref, w_ref, wx_ref, own_ref, b0, b1, b2, acc):
    r = pl.program_id(0)
    width = mine_ref.shape[1]
    nsend = b0.shape[0]

    @pl.when(r == 0)
    def _():
        acc[...] = jnp.zeros_like(acc)

    hid = lax.axis_index("hid")
    here = pl.ds(pl.multiple_of(hid * width, width), width)
    dagg = (
        lax.dot_general(mine_ref[...], w_ref[here, :], TRANS, preferred_element_type=jnp.float32)
        + lax.dot_general(other_ref[...], wx_ref[...], TRANS, preferred_element_type=jnp.float32)
    ).astype(mine_ref.dtype)
    for k in range(ntile):
        acc[cols_ref[r * ntile + k]] += lax.dot_general(
            tiles_ref[0, k], dagg, DEEP, preferred_element_type=jnp.float32
        )

    @pl.when(r == nblock - 1)
    def _():
        own_ref[...] = acc[0:nblock]
        for m, ref in enumerate((b0, b1, b2)):
            ref[...] = acc[nblock + m * nsend : nblock + (m + 1) * nsend].astype(ref.dtype)


def spread_call(tiles, cols, mine, other, weight, wx, nsend):
    nblock, ntile = tiles.shape[:2]
    width = mine.shape[1]
    rowed = pl.BlockSpec((BLK, width), lambda r, _: (r, 0))
    return pl.pallas_call(
        functools.partial(spread_kernel, ntile, nblock),
        grid_spec=pltpu.PrefetchScalarGridSpec(
            num_scalar_prefetch=1,
            grid=(nblock,),
            in_specs=[
                pl.BlockSpec((1, ntile, BLK, BLK), lambda r, _: (r, 0, 0, 0)),
                rowed,
                rowed,
                whole(weight.shape),
                whole(wx.shape),
            ],
            out_specs=[whole((nblock, BLK, width))] + [whole((nsend, BLK, width))] * 3,
            scratch_shapes=[VMEM((nblock + 3 * nsend, BLK, width), jnp.float32)],
        ),
        out_shape=[jax.ShapeDtypeStruct((nblock, BLK, width), jnp.float32)]
        + [jax.ShapeDtypeStruct((nsend, BLK, width), mine.dtype)] * 3,
        compiler_params=params(32),
        name="spread",
    )(cols, tiles, mine, other, weight, wx)


def final_kernel(sends_ref, own_ref, cotan_ref, b0, b1, b2, out_ref, acc):
    nsend = b0.shape[0]
    acc[...] = own_ref[...] + cotan_ref[...].astype(jnp.float32)
    for m, ref in enumerate((b0, b1, b2)):
        for j in range(nsend):
            acc[sends_ref[m * nsend + j]] += ref[j].astype(jnp.float32)
    out_ref[...] = acc[...].astype(out_ref.dtype)


def final_call(sends, own, cotan, backs):
    shape = own.shape
    return pl.pallas_call(
        final_kernel,
        grid_spec=pltpu.PrefetchScalarGridSpec(
            num_scalar_prefetch=1,
            grid=(1,),
            in_specs=[whole(shape)] * 2 + [whole(backs[0].shape)] * 3,
            out_specs=whole(shape),
            scratch_shapes=[VMEM(shape, jnp.float32)],
        ),
        out_shape=jax.ShapeDtypeStruct(shape, cotan.dtype),
        compiler_params=params(24),
        name="final",
    )(sends.reshape(-1), own, cotan.reshape(shape), *backs)


def body(feats, tiles, tile_cols, sends, pins, weight, bias, cotan):
    rows, width = feats.shape
    nblock = rows // BLK
    nsend = sends.shape[2]
    parts = lax.axis_size("dom")
    nbits = parts.bit_length() - 1
    shifts = (0, nbits // 2, nbits - 1)
    hid = lax.axis_index("hid")
    cols = tile_cols.reshape(-1)
    blocks = feats.reshape(nblock, BLK, width)
    picked = pick_call(blocks, sends)
    received = [swapped(picked[m], "dom", shifts[m]) for m in range(3)]
    wx = swapped(lax.dynamic_slice_in_dim(weight, (1 - hid) * width, width, 0), "hid", 0)
    agg = agg_call(tiles, cols, blocks, received)
    agg_other = swapped(agg, "hid", 0)
    out, dpre, wb = mid_call(agg, agg_other, weight, bias, pins, feats, cotan)
    dpre_other = swapped(dpre, "hid", 0)
    summed = lax.psum(wb, "dom")
    own, *outgoing = spread_call(tiles, cols, dpre, dpre_other, weight, wx, nsend)
    backs = [swapped(outgoing[m], "dom", shifts[m]) for m in range(3)]
    dfeat = final_call(sends, own, cotan, backs).reshape(rows, width)
    scale = 1.0 / math.sqrt(parts * rows)
    dweight = summed[: 2 * width] * scale
    dbias = jnp.sum(summed[2 * width :], axis=0) * scale
    return (out, dfeat, dweight, dbias)


def solution(mesh):
    return jax.shard_map(
        body,
        mesh=mesh,
        in_specs=(
            P(("basin", "dom"), "hid"),
            P(("basin", "dom"), None, None, None),
            P(("basin", "dom"), None),
            P(("basin", "dom"), None, None),
            P(("basin", "dom"), None),
            P(None, "hid"),
            P("hid"),
            P(("basin", "dom"), "hid"),
        ),
        out_specs=(
            P(("basin", "dom"), "hid"),
            P(("basin", "dom"), "hid"),
            P("basin", "hid"),
            P(("basin", "hid")),
        ),
        check_vma=False,
    )
```

time: 330 us -> 158 us (0.48)
  other arithmetic: 86.2 us -> 3.85 us
  blocking collectives: 63.6 us -> 0 us
  matrix products: 44.6 us -> 0 us
  Pallas kernels: 0 us -> 32.2 us
  local copies, waits for them, and re-layouts: 24.2 us -> 15.5 us
    scatter-add x19 -> x0, other arithmetic: 78.4 us -> none  [the longest x16 72.1 us: add_slot(): return total.at[col_slot].add(term)]
    psum x1 -> x0, blocking collectives: 61.5 us -> none  [body(): summed_weight, summed_bias = lax.psum((weight_term, bias_term), 'dom')]
    dot_general x20 -> x0, matrix products: 44.6 us -> none  [the longest x16 24.4 us: add_slot(): jnp.einsum('rij,rih->rjh', tile_slot, dblocks, preferred_element_type=jnp...]
    pallas_call x0 -> x5, Pallas kernels: none -> 32.2 us  [the longest x1 15.1 us: spread_call(): pl.pallas_call(functools.partial(spread_kernel, ntile, nblock), grid_spec...]
    all_gather x2 -> x0, waiting for transfers between devices: 18.8 us -> none  [the longest x1 9.43 us: body(): whole_agg = lax.all_gather(agg, 'hid', axis=1, tiled=True)]
    gather x4 -> x0, local copies, waits for them, and re-layouts: 14.7 us -> none  [the longest x1 9.76 us: body(): selected = sources[tile_cols]]
    unnamed x20 -> x26, local copies, waits for them, and re-layouts: 0.83 us -> 14.6 us
    psum x1, waiting for transfers between devices: 41.7 us -> 54.1 us  [body(): summed = lax.psum(wb, 'dom')]
  transfers between devices with their start and end apart: 9 -> 10, of which waited for: 6 -> 6; matrix products, arithmetic and copies ran while one was open for 4% -> 3% of each run, Pallas kernels for 0% -> 10%
where the time goes in v1:
time: 158 us; the launch traced here: 157 us
  waiting for transfers between devices  80.1 us (51%)
  Pallas kernels  32.2 us (20%)
  local copies, waits for them, and re-layouts  15.5 us (10%)
  between operations  14.1 us (9%)
  starting transfers between devices  11.3 us (7%)
  other arithmetic  3.85 us (2%)
    psum x1, waiting for transfers between devices, body(): summed = lax.psum(wb, 'dom')  54.1 us
    ppermute x9, waiting for transfers between devices, swapped(): return lax.ppermute(block, axis, route)  26 us
    pallas_call x1, Pallas kernels, spread_call(): pl.pallas_call(functools.partial(spread_kernel, ntile, nblock), grid_spec...  15.1 us
    unnamed x26, local copies, waits for them, and re-layouts  14.6 us
    ppermute x9, starting transfers between devices, swapped(): return lax.ppermute(block, axis, route)  11.3 us
    pallas_call x1, Pallas kernels, agg_call(): pl.pallas_call(functools.partial(agg_kernel, ntile, nblock, nsend), grid_...  5.9 us
    pallas_call x1, Pallas kernels, mid_call(): pl.pallas_call(mid_kernel, grid=(rows // chunk,), in_specs=[rowed, rowed,...  5.79 us
    pallas_call x1, Pallas kernels, final_call(): pl.pallas_call(final_kernel, grid_spec=pltpu.PrefetchScalarGridSpec(num_s...  3.56 us
  transfers between devices with their start and end apart: 10, of which 6 were waited for; matrix products, arithmetic and copies ran while one was open for 3% of the time, Pallas kernels for 10%

profile of v1, /device:TPU:0, one launch (start us, length us, event | category | flops | bytes accessed | tf_op | source)
XLA Modules:
  0.0 157.0 jit_solution(15859039049917356405)
XLA Ops:
  7.2 0.0 copy-start.11
  7.2 0.0 copy-start.12
  7.2 0.0 all-reduce.2.cloned.1.call-start
  7.2 0.7 reduce
  7.9 0.1 reshape.29.sends_ref
  8.0 0.0 copy-start.2
  8.0 1.2 copy-done.2
  9.2 0.0 copy-start.4
  9.2 1.8 %pick.1 = (bf16[8,128,256]{2,1,0:T(8,128)(2,1)}, bf16[8,128,256]{2,1,0:T(8,128)(2,1)}, bf16[8,128,256]{2,1,0:T(8,128)(2,1)}) custom-call(s32[24]{0:T(128)S(1)} %reshape.29.sends_ref, bf16[16,128,256]{2,1,0:T(8,128)(2,1)S(1)} %bitcast.4), custom_call_target="tpu_custom_call" | custom-call | tf_op jit(solution)/shard_map/pick/pallas_call | solution.py:44
  11.0 3.0 %collective-permute-start = (bf16[8,128,256]{2,1,0:T(8,128)(2,1)}, bf16[8,128,256]{2,1,0:T(8,128)(2,1)S(1)}, u32[]{:S(2)}, u32[]{:S(2)}) collective-permute-start(bf16[8,128,256]{2,1,0:T(8,128)(2,1)} %get-tuple-element.14), channel_id=1, source_target_pairs={{0,2},{2,0},{4,6},{6,4},{8,10},{10,8},{12,14},{14,12},{1,3},{3,1},... | collective-permute-start | bytes 1572872 | tf_op jit(solution)/shard_map/ppermute | solution.py:22
  14.0 1.6 %collective-permute-start.1 = (bf16[8,128,256]{2,1,0:T(8,128)(2,1)}, bf16[8,128,256]{2,1,0:T(8,128)(2,1)S(1)}, u32[]{:S(2)}, u32[]{:S(2)}) collective-permute-start(bf16[8,128,256]{2,1,0:T(8,128)(2,1)} %get-tuple-element.15), channel_id=1, source_target_pairs={{0,4},{4,0},{2,6},{6,2},{8,12},{12,8},{10,14},{14,10},{1,5},{5,1},... | collective-permute-start | bytes 1572872 | tf_op jit(solution)/shard_map/ppermute | solution.py:22
  15.6 2.6 %collective-permute-start.2 = (bf16[8,128,256]{2,1,0:T(8,128)(2,1)}, bf16[8,128,256]{2,1,0:T(8,128)(2,1)S(1)}, u32[]{:S(2)}, u32[]{:S(2)}) collective-permute-start(bf16[8,128,256]{2,1,0:T(8,128)(2,1)} %get-tuple-element.16), channel_id=1, source_target_pairs={{0,8},{8,0},{2,10},{10,2},{4,12},{12,4},{6,14},{14,6},{1,9},{9,1},... | collective-permute-start | bytes 1572872 | tf_op jit(solution)/shard_map/ppermute | solution.py:22
  18.2 0.8 reshape.27.cols_ref
  18.9 7.2 %collective-permute-done.r0 = bf16[8,128,256]{2,1,0:T(8,128)(2,1)S(1)} collective-permute-done((bf16[8,128,256]{2,1,0:T(8,128)(2,1)}, bf16[8,128,256]{2,1,0:T(8,128)(2,1)S(1)}, u32[]{:S(2)}, u32[]{:S(2)}) %collective-permute-start) | collective-permute-done | bytes 524320 | tf_op jit(solution)/shard_map/ppermute | solution.py:22
  26.1 12.6 %collective-permute-done.1.r1 = bf16[8,128,256]{2,1,0:T(8,128)(2,1)S(1)} collective-permute-done((bf16[8,128,256]{2,1,0:T(8,128)(2,1)}, bf16[8,128,256]{2,1,0:T(8,128)(2,1)S(1)}, u32[]{:S(2)}, u32[]{:S(2)}) %collective-permute-start.1) | collective-permute-done | bytes 524320 | tf_op jit(solution)/shard_map/ppermute | solution.py:22
  38.7 2.4 %collective-permute-done.2.r2 = bf16[8,128,256]{2,1,0:T(8,128)(2,1)S(1)} collective-permute-done((bf16[8,128,256]{2,1,0:T(8,128)(2,1)}, bf16[8,128,256]{2,1,0:T(8,128)(2,1)S(1)}, u32[]{:S(2)}, u32[]{:S(2)}) %collective-permute-start.2) | collective-permute-done | bytes 524320 | tf_op jit(solution)/shard_map/ppermute | solution.py:22
  41.1 0.0 copy-start
  41.1 3.4 %copy-done = bf16[16,16,128,128]{3,2,1,0:T(8,128)(2,1)S(1)} copy-done((bf16[16,16,128,128]{3,2,1,0:T(8,128)(2,1)S(1)}, bf16[16,16,128,128]{3,2,1,0:T(8,128)(2,1)}, u32[]{:S(2)}) %copy-start) | copy-done | bytes 8388632
  44.5 0.0 copy-start.3
  44.5 1.2 copy-done.3
  45.7 0.0 copy-start.5
  45.7 5.9 %agg.1.mine_ref = bf16[2048,256]{1,0:T(8,128)(2,1)S(1)} custom-call(s32[256]{0:T(256)S(1)} %reshape.27.cols_ref, bf16[16,16,128,128]{3,2,1,0:T(8,128)(2,1)S(1)} %copy-done, bf16[16,128,256]{2,1,0:T(8,128)(2,1)S(1)} %bitcast.5, bf16[8,128,256]{2,1,0:T(8,128)(2,1)S(1)} %collective-permute-done.r0, bf16[8,128,256]{2,1,0:T(8,128)(2,1)S(1)} %collective-permute-done.1.r1, ...), custom_call_target="tpu_custom_call" | custom-call | tf_op jit(solution)/shard_map/agg/pallas_call | solution.py:85
  51.6 0.1 collective-permute-start.3
  51.7 2.6 %collective-permute-done.3.other_ref = bf16[2048,256]{1,0:T(8,128)(2,1)S(1)} collective-permute-done((bf16[2048,256]{1,0:T(8,128)(2,1)S(1)}, bf16[2048,256]{1,0:T(8,128)(2,1)S(1)}, u32[]{:S(2)}, u32[]{:S(2)}) %collective-permute-start.3) | collective-permute-done | bytes 1048608 | tf_op jit(solution)/shard_map/ppermute | solution.py:22
  54.3 0.0 copy-done.11
  54.3 0.0 copy-done.12
  54.3 0.0 copy-done.4
  54.3 0.0 copy-done.5
  54.3 5.8 %mid.1 = (bf16[2048,256]{1,0:T(8,128)(2,1)}, bf16[2048,256]{1,0:T(8,128)(2,1)S(1)}, f32[520,256]{1,0:T(8,128)S(1)}) custom-call(bf16[2048,256]{1,0:T(8,128)(2,1)S(1)} %agg.1.mine_ref, bf16[2048,256]{1,0:T(8,128)(2,1)S(1)} %collective-permute-done.3.other_ref, bf16[512,256]{1,0:T(8,128)(2,1)S(1)} %copy-done.5, f32[1,256]{1,0:T(1,128)S(1)} %bitcast.7, ...), custom_call_target="tpu_custom_call" | custom-call | tf_op jit(solution)/shard_map/mid/pallas_call | solution.py:144
  60.1 0.0 copy-start.10
  60.1 0.8 copy-done.10
  61.0 0.1 collective-permute-start.4
  61.1 0.0 copy-start.6
  61.1 1.0 copy-done.6
  62.1 0.0 all-reduce.2.cloned.1.call-update
  62.1 0.4 collective-permute-start.5
  62.6 1.2 collective-permute-done.5.wx_ref
  63.8 0.0 collective-permute-done.4.other_ref
  63.8 0.0 copy-start.8
  63.8 1.0 copy-done.8
  64.8 0.0 copy-start.1
  64.8 3.5 %copy-done.1 = bf16[16,16,128,128]{3,2,1,0:T(8,128)(2,1)S(1)} copy-done((bf16[16,16,128,128]{3,2,1,0:T(8,128)(2,1)S(1)}, bf16[16,16,128,128]{3,2,1,0:T(8,128)(2,1)}, u32[]{:S(2)}) %copy-start.1) | copy-done | bytes 8388632
  68.3 0.0 copy-start.7
  68.3 1.2 copy-done.7
  69.5 0.0 copy-start.9
  69.5 1.2 copy-done.9
  70.8 15.1 %spread.1 = (f32[16,128,256]{2,1,0:T(8,128)S(1)}, bf16[8,128,256]{2,1,0:T(8,128)(2,1)}, bf16[8,128,256]{2,1,0:T(8,128)(2,1)}, bf16[8,128,256]{2,1,0:T(8,128)(2,1)}) custom-call(s32[256]{0:T(256)S(1)} %reshape.27.cols_ref, bf16[16,16,128,128]{3,2,1,0:T(8,128)(2,1)S(1)} %copy-done.1, bf16[2048,256]{1,0:T(8,128)(2,1)S(1)} %copy-done.7, ...), custom_call_target="tpu_custom_call" | custom-call | tf_op jit(solution)/shard_map/spread/pallas_call | solution.py:198
  85.9 0.4 collective-permute-start.6
  86.3 0.5 collective-permute-start.7
  86.8 2.6 %collective-permute-start.8 = (bf16[8,128,256]{2,1,0:T(8,128)(2,1)}, bf16[8,128,256]{2,1,0:T(8,128)(2,1)}, u32[]{:S(2)}, u32[]{:S(2)}) collective-permute-start(bf16[8,128,256]{2,1,0:T(8,128)(2,1)} %get-tuple-element.22), channel_id=1, source_target_pairs={{0,8},{8,0},{2,10},{10,2},{4,12},{12,4},{6,14},{14,6},{1,9},{9,1},... | collective-permute-start | bytes 1572872 | tf_op jit(solution)/shard_map/ppermute | solution.py:22
  89.4 54.1 %all-reduce.2.cloned.1.call-done = f32[520,256]{1,0:T(8,128)} async-done(((f32[520,256]{1,0:T(8,128)}), f32[520,256]{1,0:T(8,128)}) %all-reduce.2.cloned.1.call-update) | async-done | bytes 532496 | tf_op jit(solution)/shard_map/psum | solution.py:263
  143.4 0.7 slice_reduce_fusion
  144.2 0.6 broadcast_multiply_fusion
  144.7 1.9 %slice_multiply_fusion = f32[512,256]{1,0:T(8,128)} fusion(f32[520,256]{1,0:T(8,128)} %all-reduce.2.cloned.1.call-done), kind=kLoop, calls=%fused_computation | loop fusion | flops 131072 | bytes 1048576 | tf_op jit(solution)/shard_map/mul | solution.py:268
  146.6 0.0 collective-permute-done.6.b0
  146.6 0.0 collective-permute-done.7.b1
  146.6 0.0 collective-permute-done.8.b2
  146.6 3.6 %final.1 = bf16[16,128,256]{2,1,0:T(8,128)(2,1)} custom-call(s32[24]{0:T(128)S(1)} %reshape.29.sends_ref, f32[16,128,256]{2,1,0:T(8,128)S(1)} %get-tuple-element.19.own_ref, bf16[16,128,256]{2,1,0:T(8,128)(2,1)S(1)} %bitcast.6, bf16[8,128,256]{2,1,0:T(8,128)(2,1)} %collective-permute-done.6.b0, bf16[8,128,256]{2,1,0:T(8,128)(2,1)} %collective-permute-done.7.b1, ...), custom_call_target="tpu_custom_call" | custom-call | tf_op jit(solution)/shard_map/final/pallas_call | solution.py:231
  (1 shorter events, 0.0 us)
Async XLA Ops:
  7.2 47.2 %copy-start.11 = (f32[256]{0:T(256)S(1)}, f32[256]{0:T(256)}, u32[]{:S(2)}) copy-start(f32[256]{0:T(256)} %param.14) | copy-start | bytes 3076
  7.2 47.1 %copy-start.12 = (s32[1,32]{1,0:T(1,128)S(1)}, s32[1,32]{1,0:T(1,128)}, u32[]{:S(2)}) copy-start(s32[1,32]{1,0:T(1,128)} %pins_ref.1) | copy-start | bytes 388
  7.2 136.3 %all-reduce.2.cloned.1.call-start = ((), (), s32[]{:S(2)}) async-start(), calls=%async_computation | async-start | bytes 1064960 | tf_op jit(solution)/shard_map/psum | solution.py:263
  8.0 1.2 copy-start.2
  9.2 45.1 %copy-start.4 = (bf16[2048,256]{1,0:T(8,128)(2,1)S(1)}, bf16[2048,256]{1,0:T(8,128)(2,1)}, u32[]{:S(2)}) copy-start(bf16[2048,256]{1,0:T(8,128)(2,1)} %cotan_ref.1) | copy-start | bytes 3145732
  11.0 15.1 %collective-permute-start = (bf16[8,128,256]{2,1,0:T(8,128)(2,1)}, bf16[8,128,256]{2,1,0:T(8,128)(2,1)S(1)}, u32[]{:S(2)}, u32[]{:S(2)}) collective-permute-start(bf16[8,128,256]{2,1,0:T(8,128)(2,1)} %get-tuple-element.14), channel_id=1, source_target_pairs={{0,2},{2,0},{4,6},{6,4},{8,10},{10,8},{12,14},{14,12},{1,3},{3,1},... | collective-permute-start | bytes 1572872 | tf_op jit(solution)/shard_map/ppermute | solution.py:22
  14.0 24.7 %collective-permute-start.1 = (bf16[8,128,256]{2,1,0:T(8,128)(2,1)}, bf16[8,128,256]{2,1,0:T(8,128)(2,1)S(1)}, u32[]{:S(2)}, u32[]{:S(2)}) collective-permute-start(bf16[8,128,256]{2,1,0:T(8,128)(2,1)} %get-tuple-element.15), channel_id=1, source_target_pairs={{0,4},{4,0},{2,6},{6,2},{8,12},{12,8},{10,14},{14,10},{1,5},{5,1},... | collective-permute-start | bytes 1572872 | tf_op jit(solution)/shard_map/ppermute | solution.py:22
  15.6 25.5 %collective-permute-start.2 = (bf16[8,128,256]{2,1,0:T(8,128)(2,1)}, bf16[8,128,256]{2,1,0:T(8,128)(2,1)S(1)}, u32[]{:S(2)}, u32[]{:S(2)}) collective-permute-start(bf16[8,128,256]{2,1,0:T(8,128)(2,1)} %get-tuple-element.16), channel_id=1, source_target_pairs={{0,8},{8,0},{2,10},{10,2},{4,12},{12,4},{6,14},{14,6},{1,9},{9,1},... | collective-permute-start | bytes 1572872 | tf_op jit(solution)/shard_map/ppermute | solution.py:22
  41.1 3.4 %copy-start = (bf16[16,16,128,128]{3,2,1,0:T(8,128)(2,1)S(1)}, bf16[16,16,128,128]{3,2,1,0:T(8,128)(2,1)}, u32[]{:S(2)}) copy-start(bf16[16,16,128,128]{3,2,1,0:T(8,128)(2,1)} %tiles_ref.3) | copy-start | bytes 25165828
  44.5 1.2 copy-start.3
  45.7 8.7 %copy-start.5 = (bf16[512,256]{1,0:T(8,128)(2,1)S(1)}, bf16[512,256]{1,0:T(8,128)(2,1)}, u32[]{:S(2)}) copy-start(bf16[512,256]{1,0:T(8,128)(2,1)} %w_ref.3) | copy-start | bytes 786436
  51.6 2.7 %collective-permute-start.3 = (bf16[2048,256]{1,0:T(8,128)(2,1)S(1)}, bf16[2048,256]{1,0:T(8,128)(2,1)S(1)}, u32[]{:S(2)}, u32[]{:S(2)}) collective-permute-start(bf16[2048,256]{1,0:T(8,128)(2,1)S(1)} %agg.1.mine_ref), channel_id=1, source_target_pairs={{0,1},{1,0},{2,3},{3,2},{4,5},{5,4},{6,7},{7,6},{8,9},{9,8},{10,11... | collective-permute-start | bytes 3145736 | tf_op jit(solution)/shard_map/ppermute | solution.py:22
  60.1 0.8 copy-start.10
  61.0 2.9 %collective-permute-start.4 = (bf16[2048,256]{1,0:T(8,128)(2,1)S(1)}, bf16[2048,256]{1,0:T(8,128)(2,1)S(1)}, u32[]{:S(2)}, u32[]{:S(2)}) collective-permute-start(bf16[2048,256]{1,0:T(8,128)(2,1)S(1)} %get-tuple-element.18.mine_ref), channel_id=1, source_target_pairs={{0,1},{1,0},{2,3},{3,2},{4,5},{5,4},{6,7},{7,6},{8,9},{9,8},{10,11... | collective-permute-start | bytes 3145736 | tf_op jit(solution)/shard_map/ppermute | solution.py:22
  61.1 1.0 copy-start.6
  62.1 1.7 %collective-permute-start.5 = (bf16[256,256]{1,0:T(8,128)(2,1)S(1)}, bf16[256,256]{1,0:T(8,128)(2,1)S(1)}, u32[]{:S(2)}, u32[]{:S(2)}) collective-permute-start(bf16[256,256]{1,0:T(8,128)(2,1)S(1)} %constant_dynamic-slice_fusion), channel_id=1, source_target_pairs={{0,1},{1,0},{2,3},{3,2},{4,5},{5,4},{6,7},{7,6},{8,9},{9,8},{10,11... | collective-permute-start | bytes 393224 | tf_op jit(solution)/shard_map/ppermute | solution.py:22
  63.8 1.0 copy-start.8
  64.8 3.5 %copy-start.1 = (bf16[16,16,128,128]{3,2,1,0:T(8,128)(2,1)S(1)}, bf16[16,16,128,128]{3,2,1,0:T(8,128)(2,1)}, u32[]{:S(2)}) copy-start(bf16[16,16,128,128]{3,2,1,0:T(8,128)(2,1)} %tiles_ref.3) | copy-start | bytes 25165828
  68.3 1.2 copy-start.7
  69.5 1.2 copy-start.9
  85.9 60.7 %collective-permute-start.6 = (bf16[8,128,256]{2,1,0:T(8,128)(2,1)}, bf16[8,128,256]{2,1,0:T(8,128)(2,1)}, u32[]{:S(2)}, u32[]{:S(2)}) collective-permute-start(bf16[8,128,256]{2,1,0:T(8,128)(2,1)} %get-tuple-element.20), channel_id=1, source_target_pairs={{0,2},{2,0},{4,6},{6,4},{8,10},{10,8},{12,14},{14,12},{1,3},{3,1},... | collective-permute-start | bytes 1572872 | tf_op jit(solution)/shard_map/ppermute | solution.py:22
  86.3 60.3 %collective-permute-start.7 = (bf16[8,128,256]{2,1,0:T(8,128)(2,1)}, bf16[8,128,256]{2,1,0:T(8,128)(2,1)}, u32[]{:S(2)}, u32[]{:S(2)}) collective-permute-start(bf16[8,128,256]{2,1,0:T(8,128)(2,1)} %get-tuple-element.21), channel_id=1, source_target_pairs={{0,4},{4,0},{2,6},{6,2},{8,12},{12,8},{10,14},{14,10},{1,5},{5,1},... | collective-permute-start | bytes 1572872 | tf_op jit(solution)/shard_map/ppermute | solution.py:22
  86.8 59.8 %collective-permute-start.8 = (bf16[8,128,256]{2,1,0:T(8,128)(2,1)}, bf16[8,128,256]{2,1,0:T(8,128)(2,1)}, u32[]{:S(2)}, u32[]{:S(2)}) collective-permute-start(bf16[8,128,256]{2,1,0:T(8,128)(2,1)} %get-tuple-element.22), channel_id=1, source_target_pairs={{0,8},{8,0},{2,10},{10,2},{4,12},{12,4},{6,14},{14,6},{1,9},{9,1},... | collective-permute-start | bytes 1572872 | tf_op jit(solution)/shard_map/ppermute | solution.py:22
Sparse Core Ops, SparseCore 0:
  62.2 81.2 all-reduce.1

commit v2 on v1

--- a/solution.py
+++ b/solution.py
@@ -32,73 +32,80 @@
     )
 
 
-def pick_kernel(nsend, sends_ref, feats_ref, *out_refs):
-    for m in range(3):
+MESH = pl.DeviceIdType.MESH
+SMEM_SPEC = pl.BlockSpec(memory_space=pltpu.SMEM)
+VMEM_SPEC = pl.BlockSpec(memory_space=pltpu.VMEM)
+ANY_SPEC = pl.BlockSpec(memory_space=pl.ANY)
+
+
+def greet(partners):
+    barrier = pltpu.get_barrier_semaphore()
+    for axis, mate in partners:
+        pl.semaphore_signal(barrier, inc=1, device_id={axis: mate}, device_id_type=MESH)
+    pl.semaphore_wait(barrier, len(partners))
+
+
+def flipped(index, bit):
+    return index + (1 - 2 * ((index // (1 << bit)) % 2)) * (1 << bit)
+
+
+def front_kernel(shifts, cols_ref, sends_ref, feats_ref, tiles_ref, agg_ref, held, src, outbox, tile_sem, send_sems, recv_sems):
+    nblock, ntile = held.shape[:2]
+    nsend = outbox.shape[1]
+    me = lax.axis_index("dom")
+    fetch = pltpu.make_async_copy(tiles_ref, held, tile_sem)
+    fetch.start()
+    mates = [flipped(me, shift) for shift in shifts]
+    greet([("dom", mate) for mate in mates])
+    copies = []
+    for m in (2, 1, 0):
         for j in range(nsend):
-            out_refs[m][j] = feats_ref[sends_ref[m * nsend + j]]
-
-
-def pick_call(blocks, sends):
+            outbox[m, j] = feats_ref[sends_ref[m * nsend + j]]
+        copy = pltpu.make_async_remote_copy(
+            src_ref=outbox.at[m],
+            dst_ref=src.at[pl.ds(nblock + m * nsend, nsend)],
+            send_sem=send_sems.at[m],
+            recv_sem=recv_sems.at[m],
+            device_id={"dom": mates[m]},
+            device_id_type=MESH,
+        )
+        copy.start()
+        copies.append(copy)
+    src[0:nblock] = feats_ref[...]
+    fetch.wait()
+    for copy in copies:
+        copy.wait()
+
+    def one_row(r, carry):
+        lhs = jnp.concatenate([held[r, k] for k in range(ntile)], axis=1)
+        rhs = jnp.concatenate([src[cols_ref[r * ntile + k]] for k in range(ntile)], axis=0)
+        agg_ref[r] = jnp.dot(lhs, rhs, preferred_element_type=jnp.float32).astype(agg_ref.dtype)
+        return carry
+
+    lax.fori_loop(0, nblock, one_row, 0)
+
+
+def front_call(tiles, cols, sends, blocks, shifts):
     nblock, _, width = blocks.shape
     nsend = sends.shape[2]
     return pl.pallas_call(
-        functools.partial(pick_kernel, nsend),
-        grid_spec=pltpu.PrefetchScalarGridSpec(
-            num_scalar_prefetch=1,
-            grid=(1,),
-            in_specs=[whole((nblock, BLK, width))],
-            out_specs=[whole((nsend, BLK, width))] * 3,
-        ),
-        out_shape=[jax.ShapeDtypeStruct((nsend, BLK, width), blocks.dtype)] * 3,
-        compiler_params=params(16),
-        name="pick",
-    )(sends.reshape(-1), blocks)
-
-
-def agg_kernel(ntile, nblock, nsend, cols_ref, tiles_ref, own_ref, r0, r1, r2, agg_ref, src, sems):
-    r = pl.program_id(0)
-
-    @pl.when(r == 0)
-    def _():
-        copies = [pltpu.make_async_copy(own_ref, src.at[pl.ds(0, nblock)], sems.at[0])]
-        for m, ref in enumerate((r0, r1, r2)):
-            copies.append(
-                pltpu.make_async_copy(
-                    ref, src.at[pl.ds(nblock + m * nsend, nsend)], sems.at[m + 1]
-                )
-            )
-        for copy in copies:
-            copy.start()
-        for copy in copies:
-            copy.wait()
-
-    lhs = jnp.concatenate([tiles_ref[0, k] for k in range(ntile)], axis=1)
-    rhs = jnp.concatenate([src[cols_ref[r * ntile + k]] for k in range(ntile)], axis=0)
-    agg_ref[...] = jnp.dot(lhs, rhs, preferred_element_type=jnp.float32).astype(agg_ref.dtype)
-
-
-def agg_call(tiles, cols, blocks, received):
-    nblock, ntile = tiles.shape[:2]
-    width = blocks.shape[2]
-    nsend = received[0].shape[0]
-    anywhere = pl.BlockSpec(memory_space=pl.ANY)
-    return pl.pallas_call(
-        functools.partial(agg_kernel, ntile, nblock, nsend),
-        grid_spec=pltpu.PrefetchScalarGridSpec(
-            num_scalar_prefetch=1,
-            grid=(nblock,),
-            in_specs=[pl.BlockSpec((1, ntile, BLK, BLK), lambda r, _: (r, 0, 0, 0))]
-            + [anywhere] * 4,
-            out_specs=pl.BlockSpec((BLK, width), lambda r, _: (r, 0)),
-            scratch_shapes=[
-                VMEM((nblock + 3 * nsend, BLK, width), blocks.dtype),
-                pltpu.SemaphoreType.DMA((4,)),
-            ],
-        ),
-        out_shape=jax.ShapeDtypeStruct((nblock * BLK, width), blocks.dtype),
-        compiler_params=params(24),
-        name="agg",
-    )(cols, tiles, blocks, *received)
+        functools.partial(front_kernel, shifts),
+        in_specs=[SMEM_SPEC, SMEM_SPEC, VMEM_SPEC, ANY_SPEC],
+        out_specs=VMEM_SPEC,
+        out_shape=jax.ShapeDtypeStruct(blocks.shape, blocks.dtype),
+        scratch_shapes=[
+            VMEM(tiles.shape, tiles.dtype),
+            VMEM((nblock + 3 * nsend, BLK, width), blocks.dtype),
+            VMEM((3, nsend, BLK, width), blocks.dtype),
+            pltpu.SemaphoreType.DMA,
+            pltpu.SemaphoreType.DMA((3,)),
+            pltpu.SemaphoreType.DMA((3,)),
+        ],
+        compiler_params=pltpu.CompilerParams(
+            vmem_limit_bytes=56 << 20, collective_id=0, has_side_effects=True
+        ),
+        name="front",
+    )(cols, sends.reshape(-1), blocks, tiles)
 
 
 TRANS = (((1,), (1,)), ((), ()))
@@ -159,7 +166,7 @@
             jax.ShapeDtypeStruct((rows, width), feats.dtype),
             jax.ShapeDtypeStruct((2 * width + 8, width), jnp.float32),
         ],
-        compiler_params=params(24),
+        compiler_params=params(56),
         name="mid",
     )(mine, other, weight, bias.reshape(1, width), pins, feats, cotan)
 
@@ -212,35 +219,119 @@
         ),
         out_shape=[jax.ShapeDtypeStruct((nblock, BLK, width), jnp.float32)]
         + [jax.ShapeDtypeStruct((nsend, BLK, width), mine.dtype)] * 3,
-        compiler_params=params(32),
+        compiler_params=params(56),
         name="spread",
     )(cols, tiles, mine, other, weight, wx)
 
 
-def final_kernel(sends_ref, own_ref, cotan_ref, b0, b1, b2, out_ref, acc):
+def final_kernel(shifts, nbits, scale, inv_ref, own_ref, cotan_ref, b0, b1, b2, wb_ref, dfeat_ref, dw_ref, db_ref, acc, in0, in1, in2, wsum, outw, inw, gath, bsum, bin_, bsend, brecv, rsend, rrecv, gsend, grecv, vsend, vrecv):
+    nblock = own_ref.shape[0]
     nsend = b0.shape[0]
-    acc[...] = own_ref[...] + cotan_ref[...].astype(jnp.float32)
-    for m, ref in enumerate((b0, b1, b2)):
-        for j in range(nsend):
-            acc[sends_ref[m * nsend + j]] += ref[j].astype(jnp.float32)
-    out_ref[...] = acc[...].astype(out_ref.dtype)
-
-
-def final_call(sends, own, cotan, backs):
+    high = gath.shape[0]
+    me = lax.axis_index("dom")
+    greet([("dom", flipped(me, bit)) for bit in range(nbits)])
+
+    def push(src, dst, send, recv, bit):
+        copy = pltpu.make_async_remote_copy(
+            src_ref=src,
+            dst_ref=dst,
+            send_sem=send,
+            recv_sem=recv,
+            device_id={"dom": flipped(me, bit)},
+            device_id_type=MESH,
+        )
+        copy.start()
+        return copy
+
+    def wide(start, size):
+        return pl.ds(pl.multiple_of(start, 16), size)
+
+    boxes = (b0, b1, b2)
+    inboxes = (in0, in1, in2)
+    wsum[...] = wb_ref[0:high]
+    bsum[...] = wb_ref[high : high + 8]
+    start, size = me * 0, high
+    at = 0
+    backs = [None] * 3
+    for bit in range(nbits):
+        half = size // 2
+        upper = (me // (1 << bit)) % 2
+        give = start + (1 - upper) * half
+        start = start + upper * half
+        size = half
+        outw[at : at + half] = wsum[wide(give, half)].astype(outw.dtype)
+        copy = push(outw.at[pl.ds(at, half)], inw.at[pl.ds(at, half)], rsend.at[bit], rrecv.at[bit], bit)
+        outgoing = bsum if bit == 0 else bin_.at[2 * bit - 1]
+        bcopy = push(outgoing, bin_.at[2 * bit], vsend.at[bit], vrecv.at[bit], bit)
+        if bit == 0:
+            for m in (2, 1, 0):
+                backs[m] = push(boxes[m], inboxes[m].at[pl.ds(0, nsend)], bsend.at[m], brecv.at[m], shifts[m])
+            acc[...] = own_ref[...] + cotan_ref[...].astype(jnp.float32)
+            for m in range(3):
+                inboxes[m][nsend] = jnp.zeros(in0.shape[1:], in0.dtype)
+        copy.wait()
+        bcopy.wait()
+        here = wide(start, half)
+        wsum[here] += inw[at : at + half].astype(jnp.float32)
+        bin_[2 * bit + 1] = outgoing[...] + bin_[2 * bit]
+        at += half
+    gath[wide(start, size)] = wsum[wide(start, size)].astype(gath.dtype)
+    for bit in reversed(range(nbits)):
+        here = wide(start, size)
+        push(gath.at[here], gath.at[here], gsend.at[bit], grecv.at[bit], bit).wait()
+        start = start - ((me // (1 << bit)) % 2) * size
+        size = size * 2
+    dw_ref[...] = gath[...].astype(jnp.float32) * scale
+    db_ref[...] = jnp.sum(bin_[2 * nbits - 1], axis=0, keepdims=True) * scale
+    for m in range(3):
+        backs[m].wait()
+        for b in range(nblock):
+            total = acc[b] + inboxes[m][inv_ref[m * nblock + b]].astype(jnp.float32)
+            if m < 2:
+                acc[b] = total
+            else:
+                dfeat_ref[b] = total.astype(dfeat_ref.dtype)
+
+
+def final_call(inv, own, cotan, outgoing, wb, shifts, nbits, scale):
     shape = own.shape
+    nsend, _, width = outgoing[0].shape
+    high = wb.shape[0] - 8
+    sem = pltpu.SemaphoreType.DMA
     return pl.pallas_call(
-        final_kernel,
-        grid_spec=pltpu.PrefetchScalarGridSpec(
-            num_scalar_prefetch=1,
-            grid=(1,),
-            in_specs=[whole(shape)] * 2 + [whole(backs[0].shape)] * 3,
-            out_specs=whole(shape),
-            scratch_shapes=[VMEM(shape, jnp.float32)],
-        ),
-        out_shape=jax.ShapeDtypeStruct(shape, cotan.dtype),
-        compiler_params=params(24),
+        functools.partial(final_kernel, shifts, nbits, scale),
+        in_specs=[SMEM_SPEC] + [VMEM_SPEC] * 6,
+        out_specs=[VMEM_SPEC] * 3,
+        out_shape=[
+            jax.ShapeDtypeStruct(shape, cotan.dtype),
+            jax.ShapeDtypeStruct((high, width), jnp.float32),
+            jax.ShapeDtypeStruct((1, width), jnp.float32),
+        ],
+        scratch_shapes=[
+            VMEM(shape, jnp.float32),
+            VMEM((nsend + 1, BLK, width), cotan.dtype),
+            VMEM((nsend + 1, BLK, width), cotan.dtype),
+            VMEM((nsend + 1, BLK, width), cotan.dtype),
+            VMEM((high, width), jnp.float32),
+            VMEM((high, width), jnp.bfloat16),
+            VMEM((high, width), jnp.bfloat16),
+            VMEM((high, width), jnp.bfloat16),
+            VMEM((8, width), jnp.float32),
+            VMEM((2 * nbits, 8, width), jnp.float32),
+            sem((3,)),
+            sem((3,)),
+            sem((nbits,)),
+            sem((nbits,)),
+            sem((nbits,)),
+            sem((nbits,)),
+            sem((nbits,)),
+            sem((nbits,)),
+        ],
+        compiler_params=pltpu.CompilerParams(
+            vmem_limit_bytes=56 << 20, collective_id=1, has_side_effects=True
+        ),
         name="final",
-    )(sends.reshape(-1), own, cotan.reshape(shape), *backs)
+    )(inv, own, cotan.reshape(shape), *outgoing, wb)
 
 
 def body(feats, tiles, tile_cols, sends, pins, weight, bias, cotan):
@@ -253,21 +344,18 @@
     hid = lax.axis_index("hid")
     cols = tile_cols.reshape(-1)
     blocks = feats.reshape(nblock, BLK, width)
-    picked = pick_call(blocks, sends)
-    received = [swapped(picked[m], "dom", shifts[m]) for m in range(3)]
+    hits = sends[0][:, :, None] == jnp.arange(nblock, dtype=jnp.int32)[None, None, :]
+    ranks = jnp.arange(nsend, dtype=jnp.int32)[None, :, None] - nsend
+    inv = (nsend + jnp.sum(jnp.where(hits, ranks, 0), axis=1)).reshape(-1)
     wx = swapped(lax.dynamic_slice_in_dim(weight, (1 - hid) * width, width, 0), "hid", 0)
-    agg = agg_call(tiles, cols, blocks, received)
+    agg = front_call(tiles, cols, sends, blocks, shifts).reshape(rows, width)
     agg_other = swapped(agg, "hid", 0)
     out, dpre, wb = mid_call(agg, agg_other, weight, bias, pins, feats, cotan)
     dpre_other = swapped(dpre, "hid", 0)
-    summed = lax.psum(wb, "dom")
     own, *outgoing = spread_call(tiles, cols, dpre, dpre_other, weight, wx, nsend)
-    backs = [swapped(outgoing[m], "dom", shifts[m]) for m in range(3)]
-    dfeat = final_call(sends, own, cotan, backs).reshape(rows, width)
     scale = 1.0 / math.sqrt(parts * rows)
-    dweight = summed[: 2 * width] * scale
-    dbias = jnp.sum(summed[2 * width :], axis=0) * scale
-    return (out, dfeat, dweight, dbias)
+    dfeat, dweight, dbias = final_call(inv, own, cotan, outgoing, wb, shifts, nbits, scale)
+    return (out, dfeat.reshape(rows, width), dweight, dbias.reshape(-1))
 
 
 def solution(mesh):

time: 158 us -> 127 us (0.80)
  Pallas kernels: 32.2 us -> 110 us
  waiting for transfers between devices: 80.1 us -> 4.43 us
  between operations: 14.1 us -> 0.69 us
  starting transfers between devices: 11.3 us -> 0.71 us
  local copies, waits for them, and re-layouts: 15.5 us -> 10.5 us
  other arithmetic: 3.85 us -> 0.8 us
    pallas_call x3 -> x2, Pallas kernels: 11.2 us -> 81.3 us  [the longest x1 45.5 us: final_call(): pl.pallas_call(functools.partial(final_kernel, shifts, nbits, scale), in_...]
    psum x1 -> x0, waiting for transfers between devices: 54.1 us -> none  [body(): summed = lax.psum(wb, 'dom')]
    ppermute x9 -> x3, waiting for transfers between devices: 26 us -> 4.43 us  [swapped(): return lax.ppermute(block, axis, route)]
    ppermute x9 -> x3, starting transfers between devices: 11.3 us -> 0.71 us  [swapped(): return lax.ppermute(block, axis, route)]
    unnamed x26 -> x14, local copies, waits for them, and re-layouts: 14.6 us -> 7.95 us
    pallas_call x1, Pallas kernels: 15.1 us -> 19.4 us  [spread_call(): pl.pallas_call(functools.partial(spread_kernel, ntile, nblock), grid_spec...]
    pallas_call x1, Pallas kernels: 5.79 us -> 8.82 us  [mid_call(): pl.pallas_call(mid_kernel, grid=(rows // chunk,), in_specs=[rowed, rowed,...]
    mul x2 -> x0, other arithmetic: 2.44 us -> none  [the longest x1 1.87 us: body(): dweight = summed[:2 * width] * scale]
  transfers between devices with their start and end apart: 10 -> 3, of which waited for: 6 -> 2; matrix products, arithmetic and copies ran while one was open for 3% -> 1% of each run, Pallas kernels for 10% -> 0%
where the time goes in v2:
time: 127 us
  Pallas kernels  110 us (87%)
  local copies, waits for them, and re-layouts  10.5 us (8%)
  waiting for transfers between devices  4.43 us (3%)
    pallas_call x1, Pallas kernels, final_call(): pl.pallas_call(functools.partial(final_kernel, shifts, nbits, scale), in_...  45.5 us
    pallas_call x1, Pallas kernels, front_call(): pl.pallas_call(functools.partial(front_kernel, shifts), in_specs=[SMEM_SP...  35.8 us
    pallas_call x1, Pallas kernels, spread_call(): pl.pallas_call(functools.partial(spread_kernel, ntile, nblock), grid_spec...  19.4 us
    pallas_call x1, Pallas kernels, mid_call(): pl.pallas_call(mid_kernel, grid=(rows // chunk,), in_specs=[rowed, rowed,...  8.82 us
    unnamed x14, local copies, waits for them, and re-layouts  7.95 us
    ppermute x3, waiting for transfers between devices, swapped(): return lax.ppermute(block, axis, route)  4.43 us
  transfers between devices with their start and end apart: 3, of which 2 were waited for; matrix products, arithmetic and copies ran while one was open for 1% of the time, Pallas kernels for 0%

profile of v2, /device:TPU:0, one launch (start us, length us, event | category | flops | bytes accessed | tf_op | source)
XLA Modules:
  0.0 126.7 jit_solution(12843107898393321783)
XLA Ops:
  0.6 0.0 copy-start.4
  0.6 0.0 copy-start
  0.7 1.4 %reshape.42.cols_ref = s32[256]{0:T(256)} reshape(s32[16,16]{1,0:T(8,128)} %param.10) | data formatting | bytes 2048 | tf_op jit(solution)/shard_map/reshape | solution.py:345
  2.0 0.7 reduce
  2.7 0.6 reshape.43.sends_ref
  3.3 35.8 %front.1 = bf16[16,128,256]{2,1,0:T(8,128)(2,1)} custom-call(s32[256]{0:T(256)} %reshape.42.cols_ref, s32[24]{0:T(128)} %reshape.43.sends_ref, bf16[16,128,256]{2,1,0:T(8,128)(2,1)} %bitcast.10, bf16[16,16,128,128]{3,2,1,0:T(8,128)(2,1)} %tiles_ref.3), custom_call_target="tpu_custom_call" | custom-call | tf_op jit(solution)/shard_map/front/pallas_call | solution.py:91
  39.2 0.1 collective-permute-start
  39.2 2.9 %collective-permute-done.other_ref = bf16[2048,256]{1,0:T(8,128)(2,1)S(1)} collective-permute-done((bf16[2048,256]{1,0:T(8,128)(2,1)}, bf16[2048,256]{1,0:T(8,128)(2,1)S(1)}, u32[]{:S(2)}, u32[]{:S(2)}) %collective-permute-start) | collective-permute-done | bytes 1048608 | tf_op jit(solution)/shard_map/ppermute | solution.py:22
  42.1 0.0 copy-start.1
  42.1 1.0 copy-done.1
  43.1 8.8 %mid.1 = (bf16[2048,256]{1,0:T(8,128)(2,1)}, bf16[2048,256]{1,0:T(8,128)(2,1)}, f32[520,256]{1,0:T(8,128)}) custom-call(bf16[2048,256]{1,0:T(8,128)(2,1)} %bitcast.12, bf16[2048,256]{1,0:T(8,128)(2,1)} %copy-done.1, bf16[512,256]{1,0:T(8,128)(2,1)} %w_ref.3, f32[1,256]{1,0:T(1,128)} %bitcast.16, s32[1,32]{1,0:T(1,128)} %pins_ref.1, ...), custom_call_target="tpu_custom_call" | custom-call | tf_op jit(solution)/shard_map/mid/pallas_call | solution.py:151
  51.9 0.2 collective-permute-start.1
  52.1 0.0 copy-done
  52.1 0.4 collective-permute-start.2
  52.5 0.0 copy-done.4
  52.6 0.1 select_reduce_fusion
  52.7 0.6 add.21.inv_ref
  53.3 1.5 %collective-permute-done.2.wx_ref = bf16[256,256]{1,0:T(8,128)(2,1)S(1)} collective-permute-done((bf16[256,256]{1,0:T(8,128)(2,1)S(1)}, bf16[256,256]{1,0:T(8,128)(2,1)S(1)}, u32[]{:S(2)}, u32[]{:S(2)}) %collective-permute-start.2) | collective-permute-done | bytes 131104 | tf_op jit(solution)/shard_map/ppermute | solution.py:22
  54.8 0.0 copy-start.3
  54.8 0.0 collective-permute-done.1.other_ref
  54.8 0.6 copy-done.3
  55.5 0.0 copy-start.2
  55.5 1.0 copy-done.2
  56.4 19.4 %spread.1 = (f32[16,128,256]{2,1,0:T(8,128)}, bf16[8,128,256]{2,1,0:T(8,128)(2,1)}, bf16[8,128,256]{2,1,0:T(8,128)(2,1)}, bf16[8,128,256]{2,1,0:T(8,128)(2,1)}) custom-call(s32[256]{0:T(256)} %reshape.42.cols_ref, bf16[16,16,128,128]{3,2,1,0:T(8,128)(2,1)} %tiles_ref.3, bf16[2048,256]{1,0:T(8,128)(2,1)} %get-tuple-element.15.mine_ref, ...), custom_call_target="tpu_custom_call" | custom-call | tf_op jit(solution)/shard_map/spread/pallas_call | solution.py:205
  75.8 45.5 %final.1 = (bf16[16,128,256]{2,1,0:T(8,128)(2,1)}, f32[512,256]{1,0:T(8,128)}, f32[1,256]{1,0:T(1,128)}) custom-call(s32[48]{0:T(128)} %add.21.inv_ref, f32[16,128,256]{2,1,0:T(8,128)} %get-tuple-element.16.own_ref, bf16[16,128,256]{2,1,0:T(8,128)(2,1)} %bitcast.9, bf16[8,128,256]{2,1,0:T(8,128)(2,1)} %get-tuple-element.17.b0, ...), custom_call_target="tpu_custom_call" | custom-call | tf_op jit(solution)/shard_map/final/pallas_call | solution.py:301
  121.3 2.3 %copy.18 = bf16[2048,256]{1,0:T(8,128)(2,1)} copy(bf16[2048,256]{1,0:T(8,128)(2,1)} %bitcast.13) | data formatting | bytes 2097152
  123.6 1.9 %copy.19 = f32[512,256]{1,0:T(8,128)} copy(f32[512,256]{1,0:T(8,128)} %get-tuple-element.30) | data formatting | bytes 1048576
  125.4 1.2 copy.20
  (4 shorter events, 0.0 us)
Async XLA Ops:
  0.6 51.9 %copy-start.4 = (s32[1,3,8]{2,0,1:T(1,128)S(1)}, s32[1,3,8]{2,0,1:T(1,128)}, u32[]{:S(2)}) copy-start(s32[1,3,8]{2,0,1:T(1,128)} %param.11) | copy-start | bytes 292
  0.6 51.5 %copy-start = (bf16[512,256]{1,0:T(8,128)(2,1)S(1)}, bf16[512,256]{1,0:T(8,128)(2,1)}, u32[]{:S(2)}) copy-start(bf16[512,256]{1,0:T(8,128)(2,1)} %w_ref.3) | copy-start | bytes 786436
  39.2 2.9 %collective-permute-start = (bf16[2048,256]{1,0:T(8,128)(2,1)}, bf16[2048,256]{1,0:T(8,128)(2,1)S(1)}, u32[]{:S(2)}, u32[]{:S(2)}) collective-permute-start(bf16[2048,256]{1,0:T(8,128)(2,1)} %bitcast.11), channel_id=1, source_target_pairs={{0,1},{1,0},{2,3},{3,2},{4,5},{5,4},{6,7},{7,6},{8,9},{9,8},{10,11... | collective-permute-start | bytes 3145736 | tf_op jit(solution)/shard_map/ppermute | solution.py:22
  42.1 1.0 copy-start.1
  51.9 2.9 %collective-permute-start.1 = (bf16[2048,256]{1,0:T(8,128)(2,1)}, bf16[2048,256]{1,0:T(8,128)(2,1)S(1)}, u32[]{:S(2)}, u32[]{:S(2)}) collective-permute-start(bf16[2048,256]{1,0:T(8,128)(2,1)} %get-tuple-element.15.mine_ref), channel_id=1, source_target_pairs={{0,1},{1,0},{2,3},{3,2},{4,5},{5,4},{6,7},{7,6},{8,9},{9,8},{10,11... | collective-permute-start | bytes 3145736 | tf_op jit(solution)/shard_map/ppermute | solution.py:22
  52.1 2.7 %collective-permute-start.2 = (bf16[256,256]{1,0:T(8,128)(2,1)S(1)}, bf16[256,256]{1,0:T(8,128)(2,1)S(1)}, u32[]{:S(2)}, u32[]{:S(2)}) collective-permute-start(bf16[256,256]{1,0:T(8,128)(2,1)S(1)} %constant_dynamic-slice_fusion), channel_id=1, source_target_pairs={{0,1},{1,0},{2,3},{3,2},{4,5},{5,4},{6,7},{7,6},{8,9},{9,8},{10,11... | collective-permute-start | bytes 393224 | tf_op jit(solution)/shard_map/ppermute | solution.py:22
  54.8 0.6 copy-start.3
  55.5 1.0 copy-start.2

commit v3 on v0

v3 whole, which is shorter than its diff:
```python
import functools
import math

import jax
import jax.numpy as jnp
from jax import lax
from jax.experimental import pallas as pl
from jax.experimental.pallas import tpu as pltpu
from jax.sharding import PartitionSpec as P

BLK = 128
VMEM = pltpu.VMEM


GROUP = 4
LANES = 512


MESH = pl.DeviceIdType.MESH
SMEM_SPEC = pl.BlockSpec(memory_space=pltpu.SMEM)
VMEM_SPEC = pl.BlockSpec(memory_space=pltpu.VMEM)
ANY_SPEC = pl.BlockSpec(memory_space=pl.ANY)


def greet(partners):
    barrier = pltpu.get_barrier_semaphore()
    for axis, mate in partners:
        pl.semaphore_signal(barrier, inc=1, device_id={axis: mate}, device_id_type=MESH)
    pl.semaphore_wait(barrier, len(partners))


def flipped(index, bit):
    return index + (1 - 2 * ((index // (1 << bit)) % 2)) * (1 << bit)


def slot_tables(crow, ccol, count, pad, ntile):
    total = ccol.shape[0]

    def iota(shape, dim):
        return lax.broadcasted_iota(jnp.int32, shape, dim)

    def picked(mask, values, axis):
        return jnp.sum(jnp.where(mask, values, 0.0), axis=axis, keepdims=True)

    def groups(n):
        return jnp.floor((n + (GROUP - 1.0)) * (1.0 / GROUP))

    lanes = iota((1, LANES), 1)
    q_row = groups(picked(iota((total, LANES), 1) == ccol, 1.0, 0))
    q_col = groups(picked(iota((count, total), 0) == crow, 1.0, 1))
    base_row = picked(iota((count, LANES), 0) < iota((count, LANES), 1), q_col, 0)
    base_col = picked(iota((count, LANES), 1) < iota((count, LANES), 0), q_row, 1)
    earlier = iota((total, total), 1) < iota((total, total), 0)
    rank = picked((ccol == crow) & earlier, 1.0, 1)
    base = picked(iota((total, LANES), 1) < ccol, q_row, 1)
    pos = (base * GROUP + rank).astype(jnp.int32)
    ids = iota((total, LANES), 0).astype(jnp.float32) - pad
    index = pad + picked(iota((total, LANES), 1) == pos, ids, 0)
    block = jnp.floor(index * (1.0 / ntile))
    last = base_row + q_row
    chain = 1.0 - picked(iota((count, LANES), 1) == base_col.astype(jnp.int32), 1.0, 0)
    rows = [index, block, last, chain] + [jnp.zeros((1, LANES), jnp.float32)] * 4
    return jnp.concatenate(rows, axis=0).astype(jnp.int32)


def front_kernel(shifts, cols_ref, crow_ref, ccol_ref, sends_ref, feats_ref, tiles_ref, agg_ref, other_ref, table_ref, held, src, outbox, tile_sem, send_sems, recv_sems, hsend, hrecv):
    nblock, ntile = held.shape[:2]
    nsend = outbox.shape[1]
    me = lax.axis_index("dom")
    fetch = pltpu.make_async_copy(tiles_ref, held, tile_sem)
    fetch.start()
    mates = [flipped(me, shift) for shift in shifts]
    peer = 1 - lax.axis_index("hid")
    greet([("dom", mate) for mate in mates] + [("hid", peer)])
    copies = []
    for m in (2, 1, 0):
        for j in range(nsend):
            outbox[m, j] = feats_ref[sends_ref[m * nsend + j]]
        copy = pltpu.make_async_remote_copy(
            src_ref=outbox.at[m],
            dst_ref=src.at[pl.ds(nblock + m * nsend, nsend)],
            send_sem=send_sems.at[m],
            recv_sem=recv_sems.at[m],
            device_id={"dom": mates[m]},
            device_id_type=MESH,
        )
        copy.start()
        copies.append(copy)
    src[0:nblock] = feats_ref[...]
    table_ref[...] = slot_tables(
        crow_ref[...], ccol_ref[...], src.shape[0], nblock * ntile, ntile
    )
    fetch.wait()
    for copy in copies:
        copy.wait()

    def one_row(r, carry):
        lhs = jnp.concatenate([held[r, k] for k in range(ntile)], axis=1)
        rhs = jnp.concatenate([src[cols_ref[r * ntile + k]] for k in range(ntile)], axis=0)
        agg_ref[r] = jnp.dot(lhs, rhs, preferred_element_type=jnp.float32).astype(agg_ref.dtype)
        return carry

    swaps = []
    count = hsend.shape[0]
    for c in range(count):
        lax.fori_loop(c * nblock // count, (c + 1) * nblock // count, one_row, 0)
        span = pl.ds(c * nblock // count, nblock // count)
        swap = pltpu.make_async_remote_copy(
            src_ref=agg_ref.at[span],
            dst_ref=other_ref.at[span],
            send_sem=hsend.at[c],
            recv_sem=hrecv.at[c],
            device_id={"hid": peer},
            device_id_type=MESH,
        )
        swap.start()
        swaps.append(swap)
    for swap in swaps:
        swap.wait()


def front_call(tiles, cols, sends, blocks, shifts):
    nblock, _, width = blocks.shape
    nsend = sends.shape[2]
    return pl.pallas_call(
        functools.partial(front_kernel, shifts),
        in_specs=[SMEM_SPEC, VMEM_SPEC, VMEM_SPEC, SMEM_SPEC, VMEM_SPEC, ANY_SPEC],
        out_specs=[VMEM_SPEC] * 3,
        out_shape=[
            jax.ShapeDtypeStruct(blocks.shape, blocks.dtype),
            jax.ShapeDtypeStruct(blocks.shape, blocks.dtype),
            jax.ShapeDtypeStruct((8, LANES), jnp.int32),
        ],
        scratch_shapes=[
            VMEM(tiles.shape, tiles.dtype),
            VMEM((nblock + 3 * nsend, BLK, width), blocks.dtype),
            VMEM((3, nsend, BLK, width), blocks.dtype),
            pltpu.SemaphoreType.DMA,
            pltpu.SemaphoreType.DMA((3,)),
            pltpu.SemaphoreType.DMA((3,)),
            pltpu.SemaphoreType.DMA((4,)),
            pltpu.SemaphoreType.DMA((4,)),
        ],
        compiler_params=pltpu.CompilerParams(
            vmem_limit_bytes=56 << 20, collective_id=0, has_side_effects=True
        ),
        name="front",
    )(cols, cols.reshape(1, -1), cols.reshape(-1, 1), sends.reshape(-1), blocks, tiles)


TRANS = (((1,), (1,)), ((), ()))
DEEP = (((0,), (0,)), ((), ()))


def rear_kernel(shifts, nbits, ntile, table, inv_ref, pins_ref, mine_ref, other_ref, w_ref, bias_ref, feats_ref, cotan_ref, tiles_ref, out_ref, dfeat_ref, dw_ref, db_ref, held, buf, dagg, dpre, dother, wx, b0, b1, b2, in0, in1, in2, wsum, outw, inw, gath, bsum, btmp, fetch_sem, xsend, xrecv, hsend, hrecv, bsend, brecv, rsend, rrecv, gsend, grecv, vsend, vrecv):
    nblock, _, width = dfeat_ref.shape
    rows = nblock * BLK
    ntiles = nblock * ntile
    slots = buf.shape[0] - 1
    nsend = b0.shape[0]
    high = gath.shape[0]
    me = lax.axis_index("dom")
    hid = lax.axis_index("hid")
    peer = 1 - hid
    fetch = pltpu.make_async_copy(tiles_ref, held.at[pl.ds(0, ntiles)], fetch_sem)
    fetch.start()
    greet([("dom", flipped(me, bit)) for bit in range(nbits)] + [("hid", peer)])

    def push(src, dst, send, recv, where):
        copy = pltpu.make_async_remote_copy(
            src_ref=src,
            dst_ref=dst,
            send_sem=send,
            recv_sem=recv,
            device_id=where,
            device_id_type=MESH,
        )
        copy.start()
        return copy

    def mate(bit):
        return {"dom": flipped(me, bit)}

    def wide(start, size):
        return pl.ds(pl.multiple_of(start, 16), size)

    here = wide(hid * width, width)
    there = wide(peer * width, width)
    wcopy = push(w_ref.at[there], wx, xsend, xrecv, {"hid": peer})
    wsum[...] = jnp.zeros_like(wsum)
    bsum[...] = jnp.zeros_like(bsum)
    chunk = 256

    def middle(i, carry):
        span = wide(i * chunk, chunk)
        mine, other = mine_ref[span, :], other_ref[span, :]
        pre = (
            jnp.dot(mine, w_ref[here, :], preferred_element_type=jnp.float32)
            + jnp.dot(other, w_ref[there, :], preferred_element_type=jnp.float32)
            + bias_ref[...]
        )
        ids = lax.broadcasted_iota(jnp.int32, (chunk, pins_ref.shape[1]), 0) + i * chunk
        hit = jnp.where(ids == pins_ref[...], 1.0, 0.0)
        keep = 1.0 - jnp.max(hit, axis=1, keepdims=True)
        sig = jax.nn.sigmoid(pre)
        out_ref[span, :] = (feats_ref[span, :].astype(jnp.float32) + keep * pre * sig).astype(
            out_ref.dtype
        )
        grad = (
            keep * cotan_ref[span, :].astype(jnp.float32) * sig * (1.0 + pre * (1.0 - sig))
        ).astype(dpre.dtype)
        dpre[span, :] = grad
        wsum[here, :] += lax.dot_general(mine, grad, DEEP, preferred_element_type=jnp.float32)
        wsum[there, :] += lax.dot_general(other, grad, DEEP, preferred_element_type=jnp.float32)
        bsum[...] += jnp.sum(grad.astype(jnp.float32).reshape(chunk // 8, 8, width), axis=0)
        return carry

    nchunk = hsend.shape[0]
    part = rows // nchunk
    swaps = []
    for c in range(nchunk):
        lax.fori_loop(c * part // chunk, (c + 1) * part // chunk, middle, 0)
        span = pl.ds(c * part, part)
        swaps.append(push(dpre.at[span], dother.at[span], hsend.at[c], hrecv.at[c], {"hid": peer}))

    state = {"start": me * 0, "size": high, "at": 0}

    def reduce_start(bit):
        half = state["size"] // 2
        upper = (me // (1 << bit)) % 2
        give = state["start"] + (1 - upper) * half
        state["start"] = state["start"] + upper * half
        state["size"] = half
        at = state["at"]
        outw[at : at + half] = wsum[wide(give, half)].astype(outw.dtype)
        outgoing = bsum if bit == 0 else btmp.at[2 * bit - 1]
        return (
            push(outw.at[pl.ds(at, half)], inw.at[pl.ds(at, half)], rsend.at[bit], rrecv.at[bit], mate(bit)),
            push(outgoing, btmp.at[2 * bit], vsend.at[bit], vrecv.at[bit], mate(bit)),
        )

    def reduce_end(bit, copies):
        for copy in copies:
            copy.wait()
        half, at = state["size"], state["at"]
        wsum[wide(state["start"], half)] += inw[at : at + half].astype(jnp.float32)
        outgoing = bsum[...] if bit == 0 else btmp[2 * bit - 1]
        btmp[2 * bit + 1] = outgoing + btmp[2 * bit]
        state["at"] = at + half
        if bit == nbits - 1:
            span = wide(state["start"], half)
            gath[span] = wsum[span].astype(gath.dtype)

    def gather_start(bit):
        span = wide(state["start"], state["size"])
        return (push(gath.at[span], gath.at[span], gsend.at[bit], grecv.at[bit], mate(bit)),)

    def gather_end(bit, copies):
        for copy in copies:
            copy.wait()
        state["start"] = state["start"] - ((me // (1 << bit)) % 2) * state["size"]
        state["size"] = state["size"] * 2

    stages = [(reduce_start, reduce_end, bit) for bit in range(nbits)]
    stages += [(gather_start, gather_end, bit) for bit in reversed(range(nbits))]

    flying = stages[0][0](stages[0][2])
    dagg[nblock] = jnp.zeros(dagg.shape[1:], dagg.dtype)
    held[ntiles] = jnp.zeros(held.shape[1:], held.dtype)
    buf[0] = jnp.zeros(buf.shape[1:], buf.dtype)
    for m, ref in enumerate((in0, in1, in2)):
        ref[nsend] = jnp.zeros(ref.shape[1:], ref.dtype)
    wcopy.wait()

    def undo(r, carry):
        span = wide(r * BLK, BLK)
        dagg[r] = (
            lax.dot_general(dpre[span, :], w_ref[here, :], TRANS, preferred_element_type=jnp.float32)
            + lax.dot_general(dother[span, :], wx[...], TRANS, preferred_element_type=jnp.float32)
        ).astype(dagg.dtype)
        return carry

    for c in range(nchunk):
        swaps[c].wait()
        lax.fori_loop(c * nblock // nchunk, (c + 1) * nblock // nchunk, undo, 0)
    fetch.wait()

    def one_slot(n, carry):
        lhs = jnp.concatenate([held[table[0, n * GROUP + g]] for g in range(GROUP)], axis=0)
        rhs = jnp.concatenate([dagg[table[1, n * GROUP + g]] for g in range(GROUP)], axis=0)
        prod = lax.dot_general(lhs, rhs, DEEP, preferred_element_type=jnp.float32)
        buf[n + 1] = buf[n] * table[3, n].astype(jnp.float32) + prod
        return carry

    nstage = len(stages)
    for i in range(nstage):
        lax.fori_loop(i * slots // nstage, (i + 1) * slots // nstage, one_slot, 0)
        stages[i][1](stages[i][2], flying)
        if i + 1 < nstage:
            flying = stages[i + 1][0](stages[i + 1][2])

    boxes = (b0, b1, b2)
    inboxes = (in0, in1, in2)
    backs = [None] * 3
    for m in (2, 1, 0):
        for j in range(nsend):
            boxes[m][j] = buf[table[2, nblock + m * nsend + j]].astype(b0.dtype)
        backs[m] = push(boxes[m], inboxes[m].at[pl.ds(0, nsend)], bsend.at[m], brecv.at[m], mate(shifts[m]))
    scale = 1.0 / math.sqrt((1 << nbits) * rows)
    dw_ref[...] = gath[...].astype(jnp.float32) * scale
    db_ref[...] = jnp.sum(btmp[2 * nbits - 1], axis=0, keepdims=True) * scale
    acc = []
    for m in range(3):
        backs[m].wait()
    for b in range(nblock):
        total = buf[table[2, b]] + cotan_ref[b * BLK : (b + 1) * BLK, :].astype(jnp.float32)
        for m in range(3):
            total = total + inboxes[m][inv_ref[m * nblock + b]].astype(jnp.float32)
        dfeat_ref[b] = total.astype(dfeat_ref.dtype)


def rear_call(table, inv, pins, mine, other, weight, bias, feats, cotan, tiles, nsend, shifts, nbits):
    rows, width = feats.shape
    nblock, ntile = tiles.shape[:2]
    ntiles = nblock * ntile
    high = weight.shape[0]
    slots = (ntiles + (GROUP - 1) * (nblock + 3 * nsend)) // GROUP
    sem = pltpu.SemaphoreType.DMA
    half = feats.dtype
    return pl.pallas_call(
        functools.partial(rear_kernel, shifts, nbits, ntile),
        in_specs=[SMEM_SPEC] * 2 + [VMEM_SPEC] * 7 + [ANY_SPEC],
        out_specs=[VMEM_SPEC] * 4,
        out_shape=[
            jax.ShapeDtypeStruct((rows, width), half),
            jax.ShapeDtypeStruct((nblock, BLK, width), half),
            jax.ShapeDtypeStruct((high, width), jnp.float32),
            jax.ShapeDtypeStruct((1, width), jnp.float32),
        ],
        scratch_shapes=[
            VMEM((ntiles + 1, BLK, BLK), half),
            VMEM((slots + 1, BLK, width), jnp.float32),
            VMEM((nblock + 1, BLK, width), half),
            VMEM((rows, width), half),
            VMEM((rows, width), half),
            VMEM((width, width), half),
        ]
        + [VMEM((nsend, BLK, width), half)] * 3
        + [VMEM((nsend + 1, BLK, width), half)] * 3
        + [VMEM((high, width), jnp.float32)]
        + [VMEM((high, width), half)] * 3
        + [
            VMEM((8, width), jnp.float32),
            VMEM((2 * nbits, 8, width), jnp.float32),
            sem,
            sem,
            sem,
            sem((4,)),
            sem((4,)),
            sem((3,)),
            sem((3,)),
        ]
        + [sem((nbits,))] * 6,
        compiler_params=pltpu.CompilerParams(
            vmem_limit_bytes=60 << 20, collective_id=1, has_side_effects=True
        ),
        name="rear",
    )(
        table,
        inv,
        pins,
        mine,
        other,
        weight,
        bias.reshape(1, width),
        feats,
        cotan,
        tiles.reshape(ntiles, BLK, BLK),
    )


def body(feats, tiles, tile_cols, sends, pins, weight, bias, cotan):
    rows, width = feats.shape
    nblock = rows // BLK
    nsend = sends.shape[2]
    nbits = lax.axis_size("dom").bit_length() - 1
    shifts = (0, nbits // 2, nbits - 1)
    blocks = feats.reshape(nblock, BLK, width)
    hits = sends[0][:, :, None] == jnp.arange(nblock, dtype=jnp.int32)[None, None, :]
    ranks = jnp.arange(nsend, dtype=jnp.int32)[None, :, None] - nsend
    inv = (nsend + jnp.sum(jnp.where(hits, ranks, 0), axis=1)).reshape(-1)
    agg, other, table = front_call(tiles, tile_cols.reshape(-1), sends, blocks, shifts)
    agg, other = agg.reshape(rows, width), other.reshape(rows, width)
    out, dfeat, dweight, dbias = rear_call(
        table, inv, pins, agg, other, weight, bias, feats, cotan, tiles, nsend, shifts, nbits
    )
    return (out, dfeat.reshape(rows, width), dweight, dbias.reshape(-1))


def solution(mesh):
    return jax.shard_map(
        body,
        mesh=mesh,
        in_specs=(
            P(("basin", "dom"), "hid"),
            P(("basin", "dom"), None, None, None),
            P(("basin", "dom"), None),
            P(("basin", "dom"), None, None),
            P(("basin", "dom"), None),
            P(None, "hid"),
            P("hid"),
            P(("basin", "dom"), "hid"),
        ),
        out_specs=(
            P(("basin", "dom"), "hid"),
            P(("basin", "dom"), "hid"),
            P("basin", "hid"),
            P(("basin", "hid")),
        ),
        check_vma=False,
    )
```

time: 330 us -> 116 us (0.35)
  Pallas kernels: 0 us -> 100 us
  other arithmetic: 86.2 us -> 0.8 us
  waiting for transfers between devices: 82.7 us -> 0 us
  blocking collectives: 63.6 us -> 0 us
  matrix products: 44.6 us -> 0 us
  starting transfers between devices: 13.3 us -> 0 us
  between operations: 13.9 us -> 0.66 us
  local copies, waits for them, and re-layouts: 24.2 us -> 13.7 us
    pallas_call x0 -> x2, Pallas kernels: none -> 100 us  [the longest x1 62.6 us: rear_call(): pl.pallas_call(functools.partial(rear_kernel, shifts, nbits, ntile), in_s...]
    scatter-add x19 -> x0, other arithmetic: 78.4 us -> none  [the longest x16 72.1 us: add_slot(): return total.at[col_slot].add(term)]
    psum x1 -> x0, blocking collectives: 61.5 us -> none  [body(): summed_weight, summed_bias = lax.psum((weight_term, bias_term), 'dom')]
    dot_general x20 -> x0, matrix products: 44.6 us -> none  [the longest x16 24.4 us: add_slot(): jnp.einsum('rij,rih->rjh', tile_slot, dblocks, preferred_element_type=jnp...]
    psum x1 -> x0, waiting for transfers between devices: 41.7 us -> none  [body(): summed_weight, summed_bias = lax.psum((weight_term, bias_term), 'dom')]
    ppermute x6 -> x0, waiting for transfers between devices: 22.1 us -> none  [swapped(): return lax.ppermute(block, axis, route)]
    all_gather x2 -> x0, waiting for transfers between devices: 18.8 us -> none  [the longest x1 9.43 us: body(): whole_agg = lax.all_gather(agg, 'hid', axis=1, tiled=True)]
    gather x4 -> x0, local copies, waits for them, and re-layouts: 14.7 us -> none  [the longest x1 9.76 us: body(): selected = sources[tile_cols]]
  transfers between devices with their start and end apart: 9 -> 0, of which waited for: 6 -> 0; matrix products, arithmetic and copies ran while one was open for 4% -> 0% of each run, Pallas kernels for 0% -> 0%
where the time goes in v3:
time: 116 us; the launch traced here: 115 us
  Pallas kernels  100 us (86%)
  local copies, waits for them, and re-layouts  13.7 us (12%)
    pallas_call x1, Pallas kernels, rear_call(): pl.pallas_call(functools.partial(rear_kernel, shifts, nbits, ntile), in_s...  62.6 us
    pallas_call x1, Pallas kernels, front_call(): pl.pallas_call(functools.partial(front_kernel, shifts), in_specs=[SMEM_SP...  37.5 us
    unnamed x5, local copies, waits for them, and re-layouts  8.3 us

profile of v3, /device:TPU:0, one launch (start us, length us, event | category | flops | bytes accessed | tf_op | source)
XLA Modules:
  0.0 115.3 jit_solution(16559136268331976902)
XLA Ops:
  0.6 1.3 %reshape.45.cols_ref = s32[256]{0:T(256)} reshape(s32[16,16]{1,0:T(8,128)} %param.10) | data formatting | bytes 2048 | tf_op jit(solution)/shard_map/reshape | solution.py:392
  2.0 1.3 %reshape_reshape.6.crow_ref = s32[1,256]{1,0:T(1,128)} reshape(s32[16,16]{1,0:T(8,128)} %param.10) | data formatting | bytes 2048 | tf_op jit(solution)/shard_map/reshape;reshape | solution.py:148
  3.3 0.7 copy.16
  4.0 0.1 select_reduce_fusion
  4.1 0.7 add.18.inv_ref
  4.8 0.7 reduce
  5.5 0.6 reshape.46.sends_ref
  6.1 1.5 %reshape_reshape.8.ccol_ref = s32[256,1]{1,0:T(8,128)} reshape(s32[16,16]{1,0:T(8,128)} %param.10) | data formatting | bytes 2048 | tf_op jit(solution)/shard_map/reshape;reshape | solution.py:148
  7.5 37.5 %front.1 = (bf16[16,128,256]{2,1,0:T(8,128)(2,1)}, bf16[16,128,256]{2,1,0:T(8,128)(2,1)}, s32[8,512]{1,0:T(8,128)}) custom-call(s32[256]{0:T(256)} %reshape.45.cols_ref, s32[1,256]{1,0:T(1,128)} %reshape_reshape.6.crow_ref, s32[256,1]{1,0:T(8,128)} %reshape_reshape.8.ccol_ref, s32[24]{0:T(128)} %reshape.46.sends_ref, bf16[16,128,256]{2,1,0:T(8,128)(2,1)} %bitcast.11, ...), custom_call_target="tpu_custom_call" | custom-call | tf_op jit(solution)/shard_map/front/pallas_call | solution.py:125
  45.1 62.6 %rear.1 = (bf16[2048,256]{1,0:T(8,128)(2,1)}, bf16[16,128,256]{2,1,0:T(8,128)(2,1)}, f32[512,256]{1,0:T(8,128)}, f32[1,256]{1,0:T(1,128)}) custom-call(s32[8,512]{1,0:T(8,128)} %get-tuple-element.11.table, s32[48]{0:T(128)} %add.18.inv_ref, s32[1,32]{1,0:T(1,128)} %pins_ref.1, bf16[2048,256]{1,0:T(8,128)(2,1)} %bitcast.13, bf16[2048,256]{1,0:T(8,128)(2,1)} %bitcast.14, ...), custom_call_target="tpu_custom_call" | custom-call | tf_op jit(solution)/shard_map/rear/pallas_call | solution.py:330
  107.7 2.3 %copy.21 = bf16[2048,256]{1,0:T(8,128)(2,1)} copy(bf16[2048,256]{1,0:T(8,128)(2,1)} %get-tuple-element.22) | data formatting | bytes 2097152
  110.0 2.3 %copy.22 = bf16[2048,256]{1,0:T(8,128)(2,1)} copy(bf16[2048,256]{1,0:T(8,128)(2,1)} %bitcast.12) | data formatting | bytes 2097152
  112.2 1.9 %copy.23 = f32[512,256]{1,0:T(8,128)} copy(f32[512,256]{1,0:T(8,128)} %get-tuple-element.24) | data formatting | bytes 1048576
  114.1 1.2 %copy.24 = f32[256]{0:T(256)} copy(f32[256]{0:T(256)} %bitcast.16) | data formatting | bytes 2048
  (2 shorter events, 0.0 us)

commit v4 on v3

--- a/solution.py
+++ b/solution.py
@@ -33,8 +33,11 @@
     return index + (1 - 2 * ((index // (1 << bit)) % 2)) * (1 << bit)
 
 
-def slot_tables(crow, ccol, count, pad, ntile):
-    total = ccol.shape[0]
+def slot_tables(cols, sends_ref, count):
+    nblock, ntile = cols.shape
+    nsend = sends_ref.shape[2]
+    total = nblock * ntile
+    pad = total
 
     def iota(shape, dim):
         return lax.broadcasted_iota(jnp.int32, shape, dim)
@@ -45,7 +48,21 @@
     def groups(n):
         return jnp.floor((n + (GROUP - 1.0)) * (1.0 / GROUP))
 
+    flat = cols.astype(jnp.float32)
+    deep = jnp.where(iota((total, nblock), 0) // ntile == iota((total, nblock), 1), 1.0, 0.0)
+    wide = jnp.where(iota((ntile, total), 1) % ntile == iota((ntile, total), 0), 1.0, 0.0)
+    tall = jnp.dot(deep, flat, preferred_element_type=jnp.float32)
+    long = jnp.dot(flat, wide, preferred_element_type=jnp.float32)
+    ccol = picked(iota((total, ntile), 0) % ntile == iota((total, ntile), 1), tall, 1)
+    crow = picked(iota((nblock, total), 1) // ntile == iota((nblock, total), 0), long, 0)
+    ccol, crow = ccol.astype(jnp.int32), crow.astype(jnp.int32)
     lanes = iota((1, LANES), 1)
+    inverse = []
+    for m in range(3):
+        found = jnp.full((1, LANES), float(nsend), jnp.float32)
+        for j in range(nsend):
+            found = jnp.where(lanes == sends_ref[0, m, j], float(j), found)
+        inverse.append(found)
     q_row = groups(picked(iota((total, LANES), 1) == ccol, 1.0, 0))
     q_col = groups(picked(iota((count, total), 0) == crow, 1.0, 1))
     base_row = picked(iota((count, LANES), 0) < iota((count, LANES), 1), q_col, 0)
@@ -59,11 +76,11 @@
     block = jnp.floor(index * (1.0 / ntile))
     last = base_row + q_row
     chain = 1.0 - picked(iota((count, LANES), 1) == base_col.astype(jnp.int32), 1.0, 0)
-    rows = [index, block, last, chain] + [jnp.zeros((1, LANES), jnp.float32)] * 4
+    rows = [index, block, last, chain] + inverse + [jnp.zeros((1, LANES), jnp.float32)]
     return jnp.concatenate(rows, axis=0).astype(jnp.int32)
 
 
-def front_kernel(shifts, cols_ref, crow_ref, ccol_ref, sends_ref, feats_ref, tiles_ref, agg_ref, other_ref, table_ref, held, src, outbox, tile_sem, send_sems, recv_sems, hsend, hrecv):
+def front_kernel(shifts, cols_ref, cvec_ref, sends_ref, feats_ref, tiles_ref, agg_ref, other_ref, table_ref, held, src, outbox, tile_sem, send_sems, recv_sems, hsend, hrecv):
     nblock, ntile = held.shape[:2]
     nsend = outbox.shape[1]
     me = lax.axis_index("dom")
@@ -75,7 +92,7 @@
     copies = []
     for m in (2, 1, 0):
         for j in range(nsend):
-            outbox[m, j] = feats_ref[sends_ref[m * nsend + j]]
+            outbox[m, j] = feats_ref[sends_ref[0, m, j]]
         copy = pltpu.make_async_remote_copy(
             src_ref=outbox.at[m],
             dst_ref=src.at[pl.ds(nblock + m * nsend, nsend)],
@@ -87,16 +104,14 @@
         copy.start()
         copies.append(copy)
     src[0:nblock] = feats_ref[...]
-    table_ref[...] = slot_tables(
-        crow_ref[...], ccol_ref[...], src.shape[0], nblock * ntile, ntile
-    )
+    table_ref[...] = slot_tables(cvec_ref[...], sends_ref, src.shape[0])
     fetch.wait()
     for copy in copies:
         copy.wait()
 
     def one_row(r, carry):
         lhs = jnp.concatenate([held[r, k] for k in range(ntile)], axis=1)
-        rhs = jnp.concatenate([src[cols_ref[r * ntile + k]] for k in range(ntile)], axis=0)
+        rhs = jnp.concatenate([src[cols_ref[r, k]] for k in range(ntile)], axis=0)
         agg_ref[r] = jnp.dot(lhs, rhs, preferred_element_type=jnp.float32).astype(agg_ref.dtype)
         return carry
 
@@ -124,7 +139,7 @@
     nsend = sends.shape[2]
     return pl.pallas_call(
         functools.partial(front_kernel, shifts),
-        in_specs=[SMEM_SPEC, VMEM_SPEC, VMEM_SPEC, SMEM_SPEC, VMEM_SPEC, ANY_SPEC],
+        in_specs=[SMEM_SPEC, VMEM_SPEC, SMEM_SPEC, VMEM_SPEC, ANY_SPEC],
         out_specs=[VMEM_SPEC] * 3,
         out_shape=[
             jax.ShapeDtypeStruct(blocks.shape, blocks.dtype),
@@ -145,14 +160,14 @@
             vmem_limit_bytes=56 << 20, collective_id=0, has_side_effects=True
         ),
         name="front",
-    )(cols, cols.reshape(1, -1), cols.reshape(-1, 1), sends.reshape(-1), blocks, tiles)
+    )(cols, cols, sends, blocks, tiles)
 
 
 TRANS = (((1,), (1,)), ((), ()))
 DEEP = (((0,), (0,)), ((), ()))
 
 
-def rear_kernel(shifts, nbits, ntile, table, inv_ref, pins_ref, mine_ref, other_ref, w_ref, bias_ref, feats_ref, cotan_ref, tiles_ref, out_ref, dfeat_ref, dw_ref, db_ref, held, buf, dagg, dpre, dother, wx, b0, b1, b2, in0, in1, in2, wsum, outw, inw, gath, bsum, btmp, fetch_sem, xsend, xrecv, hsend, hrecv, bsend, brecv, rsend, rrecv, gsend, grecv, vsend, vrecv):
+def rear_kernel(shifts, nbits, ntile, table, pins_ref, mine_ref, other_ref, w_ref, bias_ref, feats_ref, cotan_ref, tiles_ref, out_ref, dfeat_ref, dw_ref, db_ref, held, buf, dagg, dpre, dother, wx, b0, b1, b2, in0, in1, in2, wsum, outw, inw, gath, bsum, btmp, fetch_sem, xsend, xrecv, hsend, hrecv, bsend, brecv, rsend, rrecv, gsend, grecv, vsend, vrecv):
     nblock, _, width = dfeat_ref.shape
     rows = nblock * BLK
     ntiles = nblock * ntile
@@ -280,9 +295,14 @@
         ).astype(dagg.dtype)
         return carry
 
+    done = 0
     for c in range(nchunk):
         swaps[c].wait()
         lax.fori_loop(c * nblock // nchunk, (c + 1) * nblock // nchunk, undo, 0)
+        if c % 2 == 1 and done + 1 < len(stages):
+            stages[done][1](stages[done][2], flying)
+            done += 1
+            flying = stages[done][0](stages[done][2])
     fetch.wait()
 
     def one_slot(n, carry):
@@ -292,12 +312,12 @@
         buf[n + 1] = buf[n] * table[3, n].astype(jnp.float32) + prod
         return carry
 
-    nstage = len(stages)
+    nstage = len(stages) - done
     for i in range(nstage):
         lax.fori_loop(i * slots // nstage, (i + 1) * slots // nstage, one_slot, 0)
-        stages[i][1](stages[i][2], flying)
+        stages[done + i][1](stages[done + i][2], flying)
         if i + 1 < nstage:
-            flying = stages[i + 1][0](stages[i + 1][2])
+            flying = stages[done + i + 1][0](stages[done + i + 1][2])
 
     boxes = (b0, b1, b2)
     inboxes = (in0, in1, in2)
@@ -315,11 +335,11 @@
     for b in range(nblock):
         total = buf[table[2, b]] + cotan_ref[b * BLK : (b + 1) * BLK, :].astype(jnp.float32)
         for m in range(3):
-            total = total + inboxes[m][inv_ref[m * nblock + b]].astype(jnp.float32)
+            total = total + inboxes[m][table[4 + m, b]].astype(jnp.float32)
         dfeat_ref[b] = total.astype(dfeat_ref.dtype)
 
 
-def rear_call(table, inv, pins, mine, other, weight, bias, feats, cotan, tiles, nsend, shifts, nbits):
+def rear_call(table, pins, mine, other, weight, bias, feats, cotan, tiles, nsend, shifts, nbits):
     rows, width = feats.shape
     nblock, ntile = tiles.shape[:2]
     ntiles = nblock * ntile
@@ -329,7 +349,7 @@
     half = feats.dtype
     return pl.pallas_call(
         functools.partial(rear_kernel, shifts, nbits, ntile),
-        in_specs=[SMEM_SPEC] * 2 + [VMEM_SPEC] * 7 + [ANY_SPEC],
+        in_specs=[SMEM_SPEC] + [VMEM_SPEC] * 7 + [ANY_SPEC],
         out_specs=[VMEM_SPEC] * 4,
         out_shape=[
             jax.ShapeDtypeStruct((rows, width), half),
@@ -367,7 +387,6 @@
         name="rear",
     )(
         table,
-        inv,
         pins,
         mine,
         other,
@@ -379,6 +398,28 @@
     )
 
 
+def emit_kernel(*refs):
+    count = len(refs) // 2
+    sems = refs[-1]
+    copies = [pltpu.make_async_copy(refs[i], refs[count + i], sems.at[i]) for i in range(count)]
+    for copy in copies:
+        copy.start()
+    for copy in copies:
+        copy.wait()
+
+
+def emit_call(*arrays):
+    count = len(arrays)
+    return pl.pallas_call(
+        emit_kernel,
+        in_specs=[ANY_SPEC] * count,
+        out_specs=[ANY_SPEC] * count,
+        out_shape=[jax.ShapeDtypeStruct(one.shape, one.dtype) for one in arrays],
+        scratch_shapes=[pltpu.SemaphoreType.DMA((count,))],
+        name="emit",
+    )(*arrays)
+
+
 def body(feats, tiles, tile_cols, sends, pins, weight, bias, cotan):
     rows, width = feats.shape
     nblock = rows // BLK
@@ -386,14 +427,12 @@
     nbits = lax.axis_size("dom").bit_length() - 1
     shifts = (0, nbits // 2, nbits - 1)
     blocks = feats.reshape(nblock, BLK, width)
-    hits = sends[0][:, :, None] == jnp.arange(nblock, dtype=jnp.int32)[None, None, :]
-    ranks = jnp.arange(nsend, dtype=jnp.int32)[None, :, None] - nsend
-    inv = (nsend + jnp.sum(jnp.where(hits, ranks, 0), axis=1)).reshape(-1)
-    agg, other, table = front_call(tiles, tile_cols.reshape(-1), sends, blocks, shifts)
+    agg, other, table = front_call(tiles, tile_cols, sends, blocks, shifts)
     agg, other = agg.reshape(rows, width), other.reshape(rows, width)
     out, dfeat, dweight, dbias = rear_call(
-        table, inv, pins, agg, other, weight, bias, feats, cotan, tiles, nsend, shifts, nbits
+        table, pins, agg, other, weight, bias, feats, cotan, tiles, nsend, shifts, nbits
     )
+    out, dfeat, dweight, dbias = emit_call(out, dfeat, dweight, dbias)
     return (out, dfeat.reshape(rows, width), dweight, dbias.reshape(-1))
 
 

time: 116 us -> 185 us (1.59)
  Pallas kernels: 100 us -> 183 us
  local copies, waits for them, and re-layouts: 13.7 us -> 1.26 us
    pallas_call x0 -> x1, Pallas kernels: none -> 80.6 us  [emit_call(): pl.pallas_call(emit_kernel, in_specs=[ANY_SPEC] * count, out_specs=[ANY_S...]
    unnamed x5 -> x1, local copies, waits for them, and re-layouts: 8.3 us -> 1.26 us
    another operation x2 -> x0, local copies, waits for them, and re-layouts: 2.79 us -> none  [the longest x1 1.45 us: front_call(): cols.reshape(-1, 1)]
    pallas_call x1, Pallas kernels: 62.6 us -> 64.9 us  [rear_call(): pl.pallas_call(functools.partial(rear_kernel, shifts, nbits, ntile), in_s...]
    reshape x2 -> x0, local copies, waits for them, and re-layouts: 1.94 us -> none  [the longest x1 1.34 us: body(): tile_cols.reshape(-1)]
where the time goes in v4:
time: 185 us
  Pallas kernels  183 us (99%)
    pallas_call x1, Pallas kernels, emit_call(): pl.pallas_call(emit_kernel, in_specs=[ANY_SPEC] * count, out_specs=[ANY_S...  80.6 us
    pallas_call x1, Pallas kernels, rear_call(): pl.pallas_call(functools.partial(rear_kernel, shifts, nbits, ntile), in_s...  64.9 us
    pallas_call x1, Pallas kernels, front_call(): pl.pallas_call(functools.partial(front_kernel, shifts), in_specs=[SMEM_SP...  37.4 us

profile of v4, /device:TPU:0, one launch (start us, length us, event | category | flops | bytes accessed | tf_op | source)
XLA Modules:
  0.0 184.8 jit_solution(8992080249343809368)
XLA Ops:
  0.6 1.3 copy.12.sends_ref
  1.9 37.4 %front.1 = (bf16[16,128,256]{2,1,0:T(8,128)(2,1)}, bf16[16,128,256]{2,1,0:T(8,128)(2,1)}, s32[8,512]{1,0:T(8,128)}) custom-call(s32[16,16]{1,0:T(8,128)} %cvec_ref.1, s32[16,16]{1,0:T(8,128)} %cvec_ref.1, s32[1,3,8]{2,1,0:T(4,128)} %copy.12.sends_ref, bf16[16,128,256]{2,1,0:T(8,128)(2,1)} %bitcast.8, bf16[16,16,128,128]{3,2,1,0:T(8,128)(2,1)} %tiles_ref.1), custom_call_target="tpu_custom_call" | custom-call | tf_op jit(solution)/shard_map/front/pallas_call | solution.py:140
  39.3 64.9 %rear.1 = (bf16[2048,256]{1,0:T(8,128)(2,1)}, bf16[16,128,256]{2,1,0:T(8,128)(2,1)}, f32[512,256]{1,0:T(8,128)}, f32[1,256]{1,0:T(1,128)}) custom-call(s32[8,512]{1,0:T(8,128)} %get-tuple-element.15.table, s32[1,32]{1,0:T(1,128)} %pins_ref.1, bf16[2048,256]{1,0:T(8,128)(2,1)} %bitcast.9, bf16[2048,256]{1,0:T(8,128)(2,1)} %bitcast.10, ...), custom_call_target="tpu_custom_call" | custom-call | tf_op jit(solution)/shard_map/rear/pallas_call | solution.py:350
  104.3 80.6 %emit.1 = (bf16[2048,256]{1,0:T(8,128)(2,1)}, bf16[16,128,256]{2,1,0:T(8,128)(2,1)}, f32[512,256]{1,0:T(8,128)}, f32[1,256]{1,0:T(1,128)}) custom-call(bf16[2048,256]{1,0:T(8,128)(2,1)} %get-tuple-element.18.refs_0_, bf16[16,128,256]{2,1,0:T(8,128)(2,1)} %get-tuple-element.19.refs_1_, f32[512,256]{1,0:T(8,128)} %get-tuple-element.20.refs_2_, ...), custom_call_target="tpu_custom_call" | custom-call | tf_op jit(solution)/shard_map/emit/pallas_call | solution.py:413

commit v5 on v4

--- a/solution.py
+++ b/solution.py
@@ -299,10 +299,6 @@
     for c in range(nchunk):
         swaps[c].wait()
         lax.fori_loop(c * nblock // nchunk, (c + 1) * nblock // nchunk, undo, 0)
-        if c % 2 == 1 and done + 1 < len(stages):
-            stages[done][1](stages[done][2], flying)
-            done += 1
-            flying = stages[done][0](stages[done][2])
     fetch.wait()
 
     def one_slot(n, carry):
@@ -398,24 +394,30 @@
     )
 
 
-def emit_kernel(*refs):
-    count = len(refs) // 2
+def emit_kernel(count, *refs):
+    given, taken, held = refs[:count], refs[count : 2 * count], refs[2 * count : 3 * count]
     sems = refs[-1]
-    copies = [pltpu.make_async_copy(refs[i], refs[count + i], sems.at[i]) for i in range(count)]
-    for copy in copies:
-        copy.start()
-    for copy in copies:
-        copy.wait()
+    reads = [pltpu.make_async_copy(given[i], held[i], sems.at[0, i]) for i in range(count)]
+    writes = [pltpu.make_async_copy(held[i], taken[i], sems.at[1, i]) for i in range(count)]
+    for read in reads:
+        read.start()
+    for read, write in zip(reads, writes):
+        read.wait()
+        write.start()
+    for write in writes:
+        write.wait()
 
 
 def emit_call(*arrays):
     count = len(arrays)
     return pl.pallas_call(
-        emit_kernel,
+        functools.partial(emit_kernel, count),
         in_specs=[ANY_SPEC] * count,
         out_specs=[ANY_SPEC] * count,
         out_shape=[jax.ShapeDtypeStruct(one.shape, one.dtype) for one in arrays],
-        scratch_shapes=[pltpu.SemaphoreType.DMA((count,))],
+        scratch_shapes=[VMEM(one.shape, one.dtype) for one in arrays]
+        + [pltpu.SemaphoreType.DMA((2, count))],
+        compiler_params=pltpu.CompilerParams(vmem_limit_bytes=56 << 20),
         name="emit",
     )(*arrays)
 

time: 185 us -> 105 us (0.57)
  Pallas kernels: 183 us -> 103 us
    pallas_call x1, Pallas kernels: 80.6 us -> 2.78 us  [emit_call(): pl.pallas_call(functools.partial(emit_kernel, count), in_specs=[ANY_SPEC]...]
    pallas_call x1, Pallas kernels: 64.9 us -> 62.7 us  [rear_call(): pl.pallas_call(functools.partial(rear_kernel, shifts, nbits, ntile), in_s...]
where the time goes in v5:
time: 105 us
  Pallas kernels  103 us (98%)
  local copies, waits for them, and re-layouts  1.26 us (1%)
    pallas_call x1, Pallas kernels, rear_call(): pl.pallas_call(functools.partial(rear_kernel, shifts, nbits, ntile), in_s...  62.7 us
    pallas_call x1, Pallas kernels, front_call(): pl.pallas_call(functools.partial(front_kernel, shifts), in_specs=[SMEM_SP...  37.4 us
    pallas_call x1, Pallas kernels, emit_call(): pl.pallas_call(functools.partial(emit_kernel, count), in_specs=[ANY_SPEC]...  2.78 us

profile of v5, /device:TPU:0, one launch (start us, length us, event | category | flops | bytes accessed | tf_op | source)
XLA Modules:
  0.0 104.8 jit_solution(14025754282023022807)
XLA Ops:
  0.6 1.3 %copy.12.sends_ref = s32[1,3,8]{2,1,0:T(4,128)} copy(s32[1,3,8]{2,0,1:T(1,128)} %param.11) | data formatting | bytes 192 | tf_op args[3]
  1.9 37.4 %front.1 = (bf16[16,128,256]{2,1,0:T(8,128)(2,1)}, bf16[16,128,256]{2,1,0:T(8,128)(2,1)}, s32[8,512]{1,0:T(8,128)}) custom-call(s32[16,16]{1,0:T(8,128)} %cvec_ref.1, s32[16,16]{1,0:T(8,128)} %cvec_ref.1, s32[1,3,8]{2,1,0:T(4,128)} %copy.12.sends_ref, bf16[16,128,256]{2,1,0:T(8,128)(2,1)} %bitcast.8, bf16[16,16,128,128]{3,2,1,0:T(8,128)(2,1)} %tiles_ref.1), custom_call_target="tpu_custom_call" | custom-call | tf_op jit(solution)/shard_map/front/pallas_call | solution.py:140
  39.3 62.7 %rear.1 = (bf16[2048,256]{1,0:T(8,128)(2,1)}, bf16[16,128,256]{2,1,0:T(8,128)(2,1)}, f32[512,256]{1,0:T(8,128)}, f32[1,256]{1,0:T(1,128)}) custom-call(s32[8,512]{1,0:T(8,128)} %get-tuple-element.15.table, s32[1,32]{1,0:T(1,128)} %pins_ref.1, bf16[2048,256]{1,0:T(8,128)(2,1)} %bitcast.9, bf16[2048,256]{1,0:T(8,128)(2,1)} %bitcast.10, ...), custom_call_target="tpu_custom_call" | custom-call | tf_op jit(solution)/shard_map/rear/pallas_call | solution.py:346
  102.0 2.8 %emit.1 = (bf16[2048,256]{1,0:T(8,128)(2,1)}, bf16[16,128,256]{2,1,0:T(8,128)(2,1)}, f32[512,256]{1,0:T(8,128)}, f32[1,256]{1,0:T(1,128)}) custom-call(bf16[2048,256]{1,0:T(8,128)(2,1)} %get-tuple-element.18.refs_0_, bf16[16,128,256]{2,1,0:T(8,128)(2,1)} %get-tuple-element.19.refs_1_, f32[512,256]{1,0:T(8,128)} %get-tuple-element.20.refs_2_, ...), custom_call_target="tpu_custom_call" | custom-call | tf_op jit(solution)/shard_map/emit/pallas_call | solution.py:413
